TPU v7x, 256 devices: a whole 4x4x8 slice. The times are simulated.
256 devices in a mesh: row: 8 (over x, core), col: 32 (over y, z).
Axes of the slice: x: 4, y: 4, z: 8, core: 2. Of those that a mesh axis runs over, the one named last changes fastest.
Arguments:
- inv_diag: float32 [2, 2048, 2048], P(None, 'row', 'col'), may hold values from -1 to 2, as said below
- coupling: float32 [2048, 2048], P('row', 'col'), may hold values from -0.125 to 0.125
- top_rhs: float32 [2, 2048, 4096], P(None, 'row', 'col'), may hold values from -6 to 6
- panel: float32 [2, 8192, 2048], P(None, 'row', 'col'), may hold values from -0.125 to 0.125
- rhs: float32 [8192, 4096], P('row', 'col'), may hold values from -6 to 6
Outputs:
- solved: float32 [2, 2048, 4096], P(None, 'row', 'col')
- trailing: float32 [8192, 4096], P('row', 'col')
Inputs may be any that keep to these rules, and one draw needn't show every extreme that they name: `inv_diag`: each of the two blocks is lower triangular with its diagonal in 1 to 2.
All inputs are finite; a program needn't handle non-finite values.
Results may differ from a plain program's by a relative error of at most 0.000073.
Values sent between devices are 32-bit elements; how exact they have to be, the bound alone decides.
A program may use at most 64 MiB of HBM per device.

v0:
```python
import jax
import jax.numpy as jnp
from jax import lax
from jax.sharding import PartitionSpec as P


def product(left, right):
    return jnp.dot(left, right, precision=lax.Precision.HIGHEST, preferred_element_type=jnp.float32)


def folder(full_rows, piece):
    return product(piece, full_rows)


def body(inv_diag, coupling, top_rhs, panel, rhs):
    first_full_rhs = lax.all_gather(top_rhs[0], "row", axis=0, tiled=True)
    solved_one = folder(first_full_rhs, lax.all_gather(inv_diag[0], "col", axis=1, tiled=True))
    full_one = lax.all_gather(solved_one, "row", axis=0, tiled=True)
    reduced = top_rhs[1] - folder(full_one, lax.all_gather(coupling, "col", axis=1, tiled=True))
    reduced_full = lax.all_gather(reduced, "row", axis=0, tiled=True)
    solved_two = folder(reduced_full, lax.all_gather(inv_diag[1], "col", axis=1, tiled=True))
    full_two = lax.all_gather(solved_two, "row", axis=0, tiled=True)
    solved = jnp.stack([solved_one, solved_two])
    stacked_full = jnp.stack([full_one, full_two])
    update = jnp.einsum(
        "krw,kwt->rt",
        lax.all_gather(panel, "col", axis=2, tiled=True),
        stacked_full,
        precision=lax.Precision.HIGHEST,
        preferred_element_type=jnp.float32,
    )
    trailing = rhs - update
    return (solved, trailing)


def solution(mesh):
    in_specs = (
        P(None, "row", "col"),
        P("row", "col"),
        P(None, "row", "col"),
        P(None, "row", "col"),
        P("row", "col"),
    )
    out_specs = (P(None, "row", "col"), P("row", "col"))
    return jax.shard_map(body, mesh=mesh, in_specs=in_specs, out_specs=out_specs, check_vma=False)
```

profile of v0, /device:TPU:1, one launch (start us, length us, event | category | flops | bytes accessed | tf_op | source)
XLA Modules:
  0.0 524.7 jit_solution(6172325524292058646)
XLA Ops:
  7.2 1.6 slice.13
  8.8 0.0 all-gather.22.cloned.1.call-start
  8.9 1.5 fusion.17
  10.5 0.7 all-gather.14.cloned.1.call-update
  11.2 29.2 %all-gather.24.cloned.1.call-done = f32[1,2048,128]{2,1,0:T(8,128)} async-done(((f32[1,256,128]{2,1,0:T(8,128)}), f32[1,2048,128]{2,1,0:T(8,128)}) %all-gather.24.cloned.1.call-update) | async-done | bytes 1048592 | tf_op jit(solution)/shard_map/all_gather | solution.py:16
  40.4 76.0 %all-gather.22.cloned.1.call-done = f32[1,256,2048]{1,2,0:T(8,128)} async-done(((f32[1,256,64]{1,2,0:T(8,128)}), f32[1,256,2048]{1,2,0:T(8,128)}) %all-gather.22.cloned.1.call-update) | async-done | bytes 2097168 | tf_op jit(solution)/shard_map/all_gather | solution.py:17
  116.4 5.9 %fusion.6 = f32[256,128]{1,0:T(8,128)} fusion(f32[1,256,2048]{1,2,0:T(8,128)} %all-gather.22.cloned.1.call-done, f32[1,2048,128]{2,1,0:T(8,128)} %all-gather.24.cloned.1.call-done), kind=kOutput, calls=%fused_computation.6 | convolution fusion | flops 805306368 | bytes 3276800 | tf_op jit(solution)/shard_map/dot_general | solution.py:8
  122.4 0.0 all-gather.26.cloned.1.call-start
  122.4 0.5 all-gather.26.cloned.1.call-update
  123.0 71.2 %all-gather.14.cloned.1.call-done = f32[256,2048]{0,1:T(8,128)} async-done(((f32[256,64]{0,1:T(8,128)}), f32[256,2048]{0,1:T(8,128)}) %all-gather.14.cloned.1.call-update) | async-done | bytes 2097168 | tf_op jit(solution)/shard_map/all_gather | solution.py:19
  194.2 30.3 %all-gather.12.cloned.1.call-done = f32[2048,128]{1,0:T(8,128)} async-done(((f32[256,128]{1,0:T(8,128)}), f32[2048,128]{1,0:T(8,128)}) %all-gather.12.cloned.1.call-update) | async-done | bytes 1048592 | tf_op jit(solution)/shard_map/all_gather | solution.py:18
  224.5 6.0 %fusion.14 = f32[256,128]{1,0:T(8,128)} fusion(f32[2048,128]{1,0:T(8,128)} %all-gather.12.cloned.1.call-done, f32[256,2048]{0,1:T(8,128)} %all-gather.14.cloned.1.call-done, f32[2,256,128]{2,1,0:T(8,128)S(1)} %copy-done.3), kind=kOutput, calls=%fused_computation.11 | convolution fusion | flops 805339136 | bytes 3407872 | tf_op jit(solution)/shard_map/dot_general | solution.py:8
  230.5 0.0 all-gather.18.cloned.1.call-start
  230.6 69.2 %all-gather.26.cloned.1.call-done = f32[1,256,2048]{1,2,0:T(8,128)} async-done(((f32[1,256,64]{1,2,0:T(8,128)}), f32[1,256,2048]{1,2,0:T(8,128)}) %all-gather.26.cloned.1.call-update) | async-done | bytes 2097168 | tf_op jit(solution)/shard_map/all_gather | solution.py:21
  299.8 30.3 %all-gather.16.cloned.1.call-done = f32[2048,128]{1,0:T(8,128)} async-done(((f32[256,128]{1,0:T(8,128)}), f32[2048,128]{1,0:T(8,128)}) %all-gather.16.cloned.1.call-update) | async-done | bytes 1048592 | tf_op jit(solution)/shard_map/all_gather | solution.py:20
  330.1 6.0 %fusion.4 = f32[128,256]{0,1:T(8,128)} fusion(f32[2048,128]{1,0:T(8,128)} %all-gather.16.cloned.1.call-done, f32[1,256,2048]{1,2,0:T(8,128)} %all-gather.26.cloned.1.call-done), kind=kOutput, calls=%fused_computation.4 | convolution fusion | flops 805306368 | bytes 3276800 | tf_op jit(solution)/shard_map/dot_general | solution.py:8
  336.1 0.2 all-gather.20.cloned.1.call-start
  336.3 0.5 all-gather.20.cloned.1.call-update
  336.9 0.2 copy.9
  337.1 1.6 pad_maximum_fusion
  338.7 23.2 %all-gather.18.cloned.1.call-done = f32[2048,128]{1,0:T(8,128)} async-done(((f32[256,128]{1,0:T(8,128)}), f32[2048,128]{1,0:T(8,128)}) %all-gather.18.cloned.1.call-update) | async-done | bytes 1048592 | tf_op jit(solution)/shard_map/all_gather | solution.py:22
  361.9 141.1 %all-gather.20.cloned.1.call-done = f32[2,1024,2048]{1,2,0:T(8,128)} async-done(((f32[2,1024,64]{1,2,0:T(8,128)}), f32[2,1024,2048]{1,2,0:T(8,128)}) %all-gather.20.cloned.1.call-update) | async-done | bytes 16777232 | tf_op jit(solution)/shard_map/all_gather | solution.py:27
  503.0 13.8 %fusion.11 = f32[1024,128]{0,1:T(8,128)S(1)} fusion(f32[1024,128]{0,1:T(8,128)S(1)} %copy.9, f32[2,1024,2048]{1,2,0:T(8,128)} %all-gather.20.cloned.1.call-done, f32[1,2048,128]{2,1,0:T(8,128)} %bitcast.35, f32[1,2048,128]{2,1,0:T(8,128)S(1)} %bitcast.31), kind=kOutput, calls=%fused_computation.9 | convolution fusion | flops 6443106304 | bytes 19922944 | tf_op jit(solution)/shard_map/krw,kwt->rt/dot_general | solution.py:25
  516.9 1.0 copy.10
  (17 shorter events, 0.3 us)
Async XLA Ops:
  7.2 217.3 %copy-start.3 = (f32[2,256,128]{2,1,0:T(8,128)S(1)}, f32[2,256,128]{2,1,0:T(8,128)}, u32[]{:S(2)}) copy-start(f32[2,256,128]{2,1,0:T(8,128)} %param.7) | copy-start | bytes 786436
  7.2 33.2 %all-gather.24.cloned.1.call-start = ((), (), s32[]{:S(2)}) async-start(), calls=%async_computation.6 | async-start | bytes 1179648 | tf_op jit(solution)/shard_map/all_gather | solution.py:16
  8.8 107.6 %all-gather.22.cloned.1.call-start = ((), (), s32[]{:S(2)}) async-start(), calls=%async_computation.5 | async-start | bytes 2162688 | tf_op jit(solution)/shard_map/all_gather | solution.py:17
  10.4 183.7 %all-gather.14.cloned.1.call-start = ((), (), s32[]{:S(2)}) async-start(), calls=%async_computation.1 | async-start | bytes 2162688 | tf_op jit(solution)/shard_map/all_gather | solution.py:19
  11.2 213.3 %all-gather.12.cloned.1.call-start = ((), (), s32[]{:S(2)}) async-start(), calls=%async_computation | async-start | bytes 1179648 | tf_op jit(solution)/shard_map/all_gather | solution.py:18
  122.4 177.4 %all-gather.26.cloned.1.call-start = ((), (), s32[]{:S(2)}) async-start(), calls=%async_computation.7 | async-start | bytes 2162688 | tf_op jit(solution)/shard_map/all_gather | solution.py:21
  123.0 207.1 %all-gather.16.cloned.1.call-start = ((), (), s32[]{:S(2)}) async-start(), calls=%async_computation.2 | async-start | bytes 1179648 | tf_op jit(solution)/shard_map/all_gather | solution.py:20
  230.5 106.4 %copy-start.2 = (f32[1024,128]{1,0:T(8,128)S(1)}, f32[1024,128]{1,0:T(8,128)}, u32[]{:S(2)}) copy-start(f32[1024,128]{1,0:T(8,128)} %param.9) | copy-start | bytes 1572868
  230.5 106.6 %copy-start.1 = (f32[256,128]{1,0:T(8,128)S(1)}, f32[256,128]{1,0:T(8,128)}, u32[]{:S(2)}) copy-start(f32[256,128]{1,0:T(8,128)} %fusion.6) | copy-start | bytes 393220
  230.5 272.5 %copy-start = (f32[2048,128]{1,0:T(8,128)S(1)}, f32[2048,128]{1,0:T(8,128)}, u32[]{:S(2)}) copy-start(f32[2048,128]{1,0:T(8,128)} %all-gather.12.cloned.1.call-done) | copy-start | bytes 3145732
  230.5 131.4 %all-gather.18.cloned.1.call-start = ((), (), s32[]{:S(2)}) async-start(), calls=%async_computation.3 | async-start | bytes 1179648 | tf_op jit(solution)/shard_map/all_gather | solution.py:22
  336.1 166.9 %all-gather.20.cloned.1.call-start = ((), (), s32[]{:S(2)}) async-start(), calls=%async_computation.4 | async-start | bytes 17301504 | tf_op jit(solution)/shard_map/all_gather | solution.py:27
Sparse Core Ops, SparseCore 0:
  10.4 29.9 all-gather.23
  43.6 72.8 all-gather.21
  119.0 75.1 all-gather.13
  196.5 27.9 all-gather.11
  226.9 72.8 all-gather.25
  302.1 27.9 all-gather.15
  336.2 25.6 all-gather.17
  364.5 138.4 all-gather.19
where the time goes:
time: 525 us
  waiting for transfers between devices  472 us (90%)
  matrix products  31.8 us (6%)
  between operations  14.2 us (3%)
    all_gather x1, waiting for transfers between devices, body(): lax.all_gather(panel, 'col', axis=2, tiled=True)  141 us
    all_gather x1, waiting for transfers between devices, body(): lax.all_gather(inv_diag[0], 'col', axis=1, tiled=True)  76 us
    all_gather x1, waiting for transfers between devices, body(): lax.all_gather(coupling, 'col', axis=1, tiled=True)  71.2 us
    all_gather x1, waiting for transfers between devices, body(): lax.all_gather(inv_diag[1], 'col', axis=1, tiled=True)  69.2 us
    all_gather x1, waiting for transfers between devices, body(): full_one = lax.all_gather(solved_one, 'row', axis=0, tiled=True)  30.3 us
    all_gather x1, waiting for transfers between devices, body(): reduced_full = lax.all_gather(reduced, 'row', axis=0, tiled=True)  30.3 us
    all_gather x1, waiting for transfers between devices, body(): first_full_rhs = lax.all_gather(top_rhs[0], 'row', axis=0, tiled=True)  29.2 us
    all_gather x1, waiting for transfers between devices, body(): full_two = lax.all_gather(solved_two, 'row', axis=0, tiled=True)  23.2 us
  transfers between devices with their start and end apart: 8, of which 8 were waited for; matrix products, arithmetic and copies ran while one was open for 3% of the time, Pallas kernels for 0%

commit v1 on v0

v1 whole, which is shorter than its diff:
```python
import jax
import jax.numpy as jnp
from jax import lax
from jax.experimental import pallas as pl
from jax.experimental.pallas import tpu as pltpu
from jax.sharding import PartitionSpec as P

MESH = pl.DeviceIdType.MESH
F32 = jnp.float32
BF16 = jnp.bfloat16
NX, NY, NZ = 4, 4, 8
KD, MD, TD = 64, 256, 128
HALF = KD // 2
CHUNKS = 4
N_COPIES = 200


def split(v):
    hi = v.astype(BF16)
    lo = (v - hi.astype(F32)).astype(BF16)
    return hi, lo


def dot(a, b):
    return jnp.dot(a, b, preferred_element_type=F32)


def dot3(hi, lo, w):
    wh, wl = split(w)
    return dot(hi, wh) + (dot(lo, wh) + dot(hi, wl))


def kernel(inv_h, cpl_h, top_h, pan_h, rhs_h, solved, trail,
           at, pt, xb, sb, rl, sh, part, r1, r2, top_v, rhs_v, send, recv, loc):
    row, col = lax.axis_index("row"), lax.axis_index("col")
    x, c = row // 2, row % 2
    y, z = col // NZ, col % NZ
    oc = 1 - c
    x_up, x_dn, x_op = (x + 1) % NX, (x + NX - 1) % NX, (x + 2) % NX
    y_up, y_dn, y_op = (y + 1) % NY, (y + NY - 1) % NY, (y + 2) % NY
    to_x_up, to_x_dn = (x_up * 2 + c, col), (x_dn * 2 + c, col)
    to_y_up, to_y_dn = (row, y_up * NZ + z), (row, y_dn * NZ + z)
    to_z_up, to_z_dn = (row, y * NZ + (z + 1) % NZ), (row, y * NZ + (z + NZ - 1) % NZ)
    to_core = (x * 2 + oc, col)

    sent = []

    class Copy:
        def __init__(self, src, dst, to, land):
            i = len(sent)
            sent.append(self)
            self.out = pltpu.make_async_remote_copy(
                src_ref=src, dst_ref=dst, send_sem=send.at[i], recv_sem=recv.at[i], device_id=to, device_id_type=MESH)
            self.into = pltpu.make_async_remote_copy(
                src_ref=land, dst_ref=land, send_sem=send.at[i], recv_sem=recv.at[i], device_id=to, device_id_type=MESH)
            self.out.start()

        def got(self):
            self.into.wait_recv()

    class ZRing:
        def __init__(self, view):
            self.view, self.step, self.live = view, 0, None

        def start(self):
            s = self.step
            up, dn = (z + NZ - s) % NZ, (z + s) % NZ
            l_up, l_dn = (z + 2 * NZ - 1 - s) % NZ, (z + 1 + s) % NZ
            a, b = self.view(up, 0), self.view(dn, 1)
            self.live = (Copy(a, a, to_z_up, self.view(l_up, 0)), Copy(b, b, to_z_dn, self.view(l_dn, 1)))

        def advance(self):
            for copy in self.live:
                copy.got()
            self.step += 1
            if self.step < NZ - 1:
                self.start()
            return self.step == NZ - 1

    class YGather:
        def __init__(self, view):
            v = self.view = view
            self.up0 = Copy(v(y, 0), v(y, 0), to_y_up, v(y_dn, 0))
            self.dn1 = Copy(v(y, 1), v(y, 1), to_y_dn, v(y_up, 1))
            self.up1 = Copy(v(y, 1), v(y, 1), to_y_up, v(y_dn, 1))
            self.dn0 = Copy(v(y, 0), v(y, 0), to_y_dn, v(y_up, 0))

        def forward(self):
            v = self.view
            self.up0.got()
            self.f0 = Copy(v(y_dn, 0), v(y_dn, 0), to_y_up, v(y_op, 0))
            self.dn1.got()
            self.f1 = Copy(v(y_up, 1), v(y_up, 1), to_y_dn, v(y_op, 1))

        def finish(self):
            for copy in (self.up1, self.dn0, self.f0, self.f1):
                copy.got()

    class XGather:
        def __init__(self, b):
            self.b = b
            me, other = xb.at[b, row], xb.at[b, x * 2 + oc]
            up, dn = xb.at[b, x_up * 2 + c], xb.at[b, x_dn * 2 + c]
            self.up = Copy(me, me, to_x_up, dn)
            self.dn = Copy(me, me, to_x_dn, up)
            self.own = Copy(me, me, to_core, other)

        def forward(self):
            b = self.b
            up, dn = xb.at[b, x_up * 2 + c], xb.at[b, x_dn * 2 + c]
            half = TD // 2
            self.up.got()
            s = xb.at[b, x_dn * 2 + c, pl.ds(0, half)]
            self.f0 = Copy(s, s, to_x_up, xb.at[b, x_op * 2 + c, pl.ds(0, half)])
            self.dn.got()
            s = xb.at[b, x_up * 2 + c, pl.ds(half, half)]
            self.f1 = Copy(s, s, to_x_dn, xb.at[b, x_op * 2 + c, pl.ds(half, half)])
            self.c0 = Copy(dn, dn, to_core, xb.at[b, x_dn * 2 + oc])
            self.c1 = Copy(up, up, to_core, xb.at[b, x_up * 2 + oc])

        def finish(self):
            b = self.b
            self.f0.got()
            self.f1.got()
            s = xb.at[b, x_op * 2 + c]
            self.c2 = Copy(s, s, to_core, xb.at[b, x_op * 2 + oc])

        def close(self):
            for copy in (self.own, self.c0, self.c1, self.c2):
                copy.got()

    class YSwap:
        def __init__(self, k, b):
            self.k, self.b = k, b
            half = TD // 2
            op = y_op * 2 + c
            self.r0 = Copy(xb.at[b, op, pl.ds(0, half)], rl.at[k, 0], to_y_up, rl.at[k, 0])
            self.r1 = Copy(xb.at[b, op, pl.ds(half, half)], rl.at[k, 1], to_y_dn, rl.at[k, 1])
            self.up = Copy(xb.at[b, y_up * 2 + c], sb.at[k, c, y], to_y_up, sb.at[k, c, y_dn])
            self.dn = Copy(xb.at[b, y_dn * 2 + c], sb.at[k, c, y], to_y_dn, sb.at[k, c, y_up])

        def forward(self):
            k = self.k
            half = TD // 2
            self.r0.got()
            self.f0 = Copy(rl.at[k, 0], sb.at[k, c, y_dn, pl.ds(0, half)], to_y_up, sb.at[k, c, y_op, pl.ds(0, half)])
            self.r1.got()
            self.f1 = Copy(rl.at[k, 1], sb.at[k, c, y_up, pl.ds(half, half)], to_y_dn,
                           sb.at[k, c, y_op, pl.ds(half, half)])
            self.up.got()
            s = sb.at[k, c, y_dn]
            self.c0 = Copy(s, s, to_core, sb.at[k, oc, y_dn])
            self.dn.got()
            s = sb.at[k, c, y_up]
            self.c1 = Copy(s, s, to_core, sb.at[k, oc, y_up])

        def finish(self):
            k = self.k
            self.f0.got()
            self.f1.got()
            s = sb.at[k, c, y_op]
            self.c2 = Copy(s, s, to_core, sb.at[k, oc, y_op])
            for cc in range(2):
                hi, lo = split(xb[self.b, y * 2 + cc])
                sh[k, cc, 0, y] = hi
                sh[k, cc, 1, y] = lo
            for yy in (y_dn, y_up, y_op):
                hi, lo = split(sb[k, c, yy])
                sh[k, c, 0, yy] = hi
                sh[k, c, 1, yy] = lo
            for copy in (self.c0, self.c1, self.c2):
                copy.got()
            for yy in (y_dn, y_up, y_op):
                hi, lo = split(sb[k, oc, yy])
                sh[k, oc, 0, yy] = hi
                sh[k, oc, 1, yy] = lo

    def solve(a, b):
        total = jnp.zeros((TD, MD), F32)
        for r in range(2 * NX):
            hi, lo = split(xb[b, r])
            w = at[a, r // 2, (r % 2) * 4:(r % 2) * 4 + 4].reshape(MD, MD)
            total = total + dot3(hi, lo, w)
        return total

    def partial(j, k):
        total = jnp.zeros((NY * TD, MD), F32)
        for cc in range(2):
            w = pt[j, k, 4 * cc:4 * cc + 4].reshape(MD, MD)
            hi = sh[k, cc, 0].reshape(NY * TD, MD)
            lo = sh[k, cc, 1].reshape(NY * TD, MD)
            total = total + dot3(hi, lo, w)
        return total.reshape(NY, TD, MD)

    class YSum:
        def __init__(self, j):
            self.j = j
            half = TD // 2
            self.a0 = Copy(part.at[j, y_op, pl.ds(0, half)], r1.at[j, 0], to_y_up, r1.at[j, 0])
            self.a1 = Copy(part.at[j, y_op, pl.ds(half, half)], r1.at[j, 1], to_y_dn, r1.at[j, 1])

        def forward(self):
            j = self.j
            half = TD // 2
            self.a0.got()
            part[j, y_up, pl.ds(0, half)] = part[j, y_up, pl.ds(0, half)] + r1[j, 0]
            self.b0 = Copy(part.at[j, y_up], r2.at[j, 0], to_y_up, r2.at[j, 0])
            self.a1.got()
            part[j, y_dn, pl.ds(half, half)] = part[j, y_dn, pl.ds(half, half)] + r1[j, 1]
            self.b1 = Copy(part.at[j, y_dn], r2.at[j, 1], to_y_dn, r2.at[j, 1])

        def finish(self):
            j = self.j
            self.b0.got()
            self.b1.got()
            total = part[j, y] + (r2[j, 0] + r2[j, 1])
            rows = pl.ds(j * MD, MD)
            trail[rows] = rhs_v[rows] - total.T

    local = []

    def bring(src, dst):
        copy = pltpu.make_async_copy(src, dst, loc.at[len(local)])
        local.append(copy)
        copy.start()
        return copy

    bring(inv_h.at[0], at.at[0, y, z])
    bring(cpl_h, at.at[1, y, z])
    bring(inv_h.at[1], at.at[2, y, z])
    bring(top_h, top_v)
    for j in range(CHUNKS):
        bring(pan_h.at[:, :, pl.ds(j * MD, MD)], pt.at[j, :, z])
    bring(rhs_h, rhs_v)

    barrier = pltpu.get_barrier_semaphore()
    peers = (to_x_up, to_x_dn, to_y_up, to_y_dn, to_z_up, to_z_dn, to_core)
    for peer in peers:
        pl.semaphore_signal(barrier, inc=1, device_id=peer, device_id_type=MESH)
    pl.semaphore_wait(barrier, len(peers))

    local[0].wait()
    gather_a0 = YGather(lambda yy, h: at.at[0, yy, z, pl.ds(h * HALF, HALF)])
    local[1].wait()
    local[2].wait()
    ring_ca = ZRing(lambda zz, h: at.at[pl.ds(1, 2), y, zz, pl.ds(h * HALF, HALF)])
    ring_ca.start()
    local[3].wait()
    xb[0, row] = top_v[0].T
    gx0 = XGather(0)
    gather_a0.forward()
    ring_ca.advance()
    gather_a0.finish()
    ring_a0 = ZRing(lambda zz, h: at.at[0, :, zz, pl.ds(h * HALF, HALF)])
    ring_a0.start()
    gx0.forward()
    ring_ca.advance()
    ring_a0.advance()
    gx0.finish()
    ring_ca.advance()
    ring_ca.advance()
    ring_a0.advance()
    gx0.close()
    ring_ca.advance()
    ring_ca.advance()
    ring_a0.advance()
    ring_ca.advance()
    gather_c = YGather(lambda yy, h: at.at[1, yy, :, pl.ds(h * HALF, HALF)])
    ring_a0.advance()
    ring_a0.advance()
    gather_c.forward()
    gather_a1 = YGather(lambda yy, h: at.at[2, yy, :, pl.ds(h * HALF, HALF)])
    for copy in local[4:]:
        copy.wait()
    rings = [ZRing(lambda zz, h, j=j: pt.at[j, :, zz, pl.ds(h * HALF, HALF)]) for j in range(CHUNKS)]
    rings[0].start()
    ring_a0.advance()
    rings[1].start()
    ring_a0.advance()

    def service(pair):
        rings[2 * pair].advance()
        return rings[2 * pair + 1].advance()

    first = solve(0, 0)
    xb[1, row] = first
    gx1 = XGather(1)
    solved[0] = first.T
    service(0)
    gather_c.finish()
    gx1.forward()
    service(0)
    gx1.finish()
    gx1.close()
    service(0)
    reduced = top_v[1].T - solve(1, 1)
    xb[2, row] = reduced
    gx2 = XGather(2)
    gather_a1.forward()
    service(0)
    gx2.forward()
    swap0 = YSwap(0, 1)
    service(0)
    gx2.finish()
    gather_a1.finish()
    gx2.close()
    service(0)
    second = solve(2, 2)
    xb[3, row] = second
    gx3 = XGather(3)
    solved[1] = second.T
    service(0)
    rings[2].start()
    rings[3].start()
    gx3.forward()
    swap0.forward()
    swap0.finish()
    for j in (0, 1):
        part[j] = partial(j, 0)
    gx3.finish()
    service(1)
    gx3.close()
    swap1 = YSwap(1, 3)
    service(1)
    swap1.forward()
    service(1)
    swap1.finish()
    sums = []
    for j in (0, 1):
        part[j] = part[j] + partial(j, 1)
        sums.append(YSum(j))
        service(1)
    sums[0].forward()
    service(1)
    sums[1].forward()
    service(1)
    for j in (2, 3):
        part[j] = partial(j, 0) + partial(j, 1)
        sums.append(YSum(j))
    for s in sums[2:]:
        s.forward()
    for s in sums:
        s.finish()
    for copy in sent:
        copy.out.wait_send()


def body(inv_diag, coupling, top_rhs, panel, rhs):
    hbm = pl.BlockSpec(memory_space=pl.ANY)
    vmem = pl.BlockSpec(memory_space=pltpu.VMEM)
    solved, trailing = pl.pallas_call(
        kernel,
        out_shape=(jax.ShapeDtypeStruct((2, MD, TD), F32), jax.ShapeDtypeStruct((CHUNKS * MD, TD), F32)),
        in_specs=[hbm] * 5,
        out_specs=(vmem, vmem),
        scratch_shapes=[
            pltpu.VMEM((3, NY, NZ, KD, MD), F32),
            pltpu.VMEM((CHUNKS, 2, NZ, KD, MD), F32),
            pltpu.VMEM((4, 2 * NX, TD, MD), F32),
            pltpu.VMEM((2, 2, NY, TD, MD), F32),
            pltpu.VMEM((2, 2, TD // 2, MD), F32),
            pltpu.VMEM((2, 2, 2, NY, TD, MD), BF16),
            pltpu.VMEM((CHUNKS, NY, TD, MD), F32),
            pltpu.VMEM((CHUNKS, 2, TD // 2, MD), F32),
            pltpu.VMEM((CHUNKS, 2, TD, MD), F32),
            pltpu.VMEM((2, MD, TD), F32),
            pltpu.VMEM((CHUNKS * MD, TD), F32),
            pltpu.SemaphoreType.DMA((N_COPIES,)),
            pltpu.SemaphoreType.DMA((N_COPIES,)),
            pltpu.SemaphoreType.DMA((16,)),
        ],
        compiler_params=pltpu.CompilerParams(
            collective_id=0, has_side_effects=True, vmem_limit_bytes=48 * 1024 * 1024),
    )(jnp.swapaxes(inv_diag, 1, 2), coupling.T, top_rhs, jnp.swapaxes(panel, 1, 2), rhs)
    return solved, trailing


def solution(mesh):
    in_specs = (
        P(None, "row", "col"),
        P("row", "col"),
        P(None, "row", "col"),
        P(None, "row", "col"),
        P("row", "col"),
    )
    out_specs = (P(None, "row", "col"), P("row", "col"))
    return jax.shard_map(body, mesh=mesh, in_specs=in_specs, out_specs=out_specs, check_vma=False)
```

time: 525 us -> 142 us (0.27)
  waiting for transfers between devices: 472 us -> 0 us
  Pallas kernels: 0 us -> 135 us
  matrix products: 31.8 us -> 0 us
  between operations: 14.2 us -> 0.65 us
    all_gather x8 -> x0, waiting for transfers between devices: 470 us -> none  [the longest x1 141 us: body(): lax.all_gather(panel, 'col', axis=2, tiled=True)]
    pallas_call x0 -> x1, Pallas kernels: none -> 135 us  [body(): pl.pallas_call(kernel, out_shape=(jax.ShapeDtypeStruct((2, MD, TD), F32),...]
    dot_general x4 -> x0, matrix products: 31.8 us -> none  [the longest x3 17.9 us: product(): jnp.dot(left, right, precision=lax.Precision.HIGHEST, preferred_element_t...]
  transfers between devices with their start and end apart: 8 -> 0, of which waited for: 8 -> 0; matrix products, arithmetic and copies ran while one was open for 3% -> 0% of each run, Pallas kernels for 0% -> 0%
where the time goes in v1:
time: 142 us; the launch traced here: 141 us
  Pallas kernels  135 us (95%)
  local copies, waits for them, and re-layouts  6.27 us (4%)
    pallas_call x1, Pallas kernels, body(): pl.pallas_call(kernel, out_shape=(jax.ShapeDtypeStruct((2, MD, TD), F32),...  135 us
    unnamed x12, local copies, waits for them, and re-layouts  6.27 us

profile of v1, /device:TPU:1, one launch (start us, length us, event | category | flops | bytes accessed | tf_op | source)
XLA Modules:
  0.0 141.4 jit_solution(5916879663162927977)
XLA Ops:
  0.6 0.0 copy-start
  0.6 1.0 copy-done
  1.7 0.0 copy-start.1
  1.7 1.0 copy-done.1
  2.7 0.0 copy-start.2
  2.7 0.9 copy-done.2
  3.7 0.0 copy-start.3
  3.7 0.9 copy-done.3
  4.6 0.0 copy-start.4
  4.6 0.8 copy-done.4
  5.4 134.5 %shard_map.68 = (f32[2,256,128]{2,1,0:T(8,128)S(1)}, f32[1024,128]{1,0:T(8,128)S(1)}) custom-call(f32[2,64,256]{2,1,0:T(8,128)S(1)} %bitcast.4, f32[64,256]{1,0:T(8,128)S(1)} %bitcast.5, f32[2,256,128]{2,1,0:T(8,128)S(1)} %copy-done.2, f32[2,64,1024]{2,1,0:T(8,128)S(1)} %bitcast.3, f32[1024,128]{1,0:T(8,128)S(1)} %copy-done.1), custom_call_target="tpu_custom_call" | custom-call | tf_op jit(solution)/shard_map/pallas_call | solution.py:351
  139.9 0.7 copy.9
  140.6 0.8 copy.10
Async XLA Ops:
  0.6 1.0 copy-start
  1.7 1.0 copy-start.1
  2.7 0.9 copy-start.2
  3.7 0.9 copy-start.3
  4.6 0.8 copy-start.4

commit v2 on v0

v2 whole, which is shorter than its diff:
```python
import jax
import jax.numpy as jnp
from jax import lax
from jax.experimental import pallas as pl
from jax.experimental.pallas import tpu as pltpu
from jax.sharding import PartitionSpec as P

MESH = pl.DeviceIdType.MESH
F32 = jnp.float32
BF16 = jnp.bfloat16
NX, NY, NZ = 4, 4, 8
KD, MD, TD = 64, 256, 128
KH, TH = KD // 2, TD // 2
CHUNKS = 4
N_COPIES = 240


def split(v):
    hi = v.astype(BF16)
    lo = (v - hi.astype(F32)).astype(BF16)
    return hi, lo


def dot(a, b):
    return jnp.dot(a, b, preferred_element_type=F32)


def dot3(hi, lo, w):
    wh, wl = split(w)
    return dot(hi, wh) + (dot(lo, wh) + dot(hi, wl))


def kernel(inv_h, cpl_h, top_h, pan_h, rhs_h, solved, trail,
           az, a1, pt, xm, sb, sh, xr, part, r1, r2, top_v, rhs_v, send, recv, arrive, loc):
    row, col = lax.axis_index("row"), lax.axis_index("col")
    x, c = row // 2, row % 2
    y, z = col // NZ, col % NZ
    oc = 1 - c
    x_up, x_dn, x_op = (x + 1) % NX, (x + NX - 1) % NX, (x + 2) % NX
    y_up, y_dn, y_op = (y + 1) % NY, (y + NY - 1) % NY, (y + 2) % NY
    to_x_up, to_x_dn = (x_up * 2 + c, col), (x_dn * 2 + c, col)
    to_y_up, to_y_dn, to_y_op = (row, y_up * NZ + z), (row, y_dn * NZ + z), (row, y_op * NZ + z)
    to_z_up, to_z_dn = (row, y * NZ + (z + 1) % NZ), (row, y * NZ + (z + NZ - 1) % NZ)
    to_core = (x * 2 + oc, col)
    halves = (pl.ds(0, TH), pl.ds(TH, TH))

    sent = []

    class Copy:
        def __init__(self, src, dst, to, land):
            i = len(sent)
            self.out = pltpu.make_async_remote_copy(
                src_ref=src, dst_ref=dst, send_sem=send.at[i], recv_sem=recv.at[i], device_id=to, device_id_type=MESH)
            self.into = pltpu.make_async_remote_copy(
                src_ref=land, dst_ref=land, send_sem=send.at[i], recv_sem=recv.at[i], device_id=to, device_id_type=MESH)
            sent.append((self.out, None))
            self.out.start()

        def got(self):
            self.into.wait_recv()

    def same(view, at, to, land):
        return Copy(view(at), view(at), to, view(land))

    class ZRing:
        def __init__(self, full, half):
            self.full, self.half, self.hop = full, half, 0

        def start(self):
            s = self.hop
            up, dn = (z + NZ - s) % NZ, (z + s) % NZ
            l_up, l_dn = (z + NZ - 1 - s) % NZ, (z + 1 + s) % NZ
            if s < 3:
                self.live = (same(self.full, up, to_z_up, l_up), same(self.full, dn, to_z_dn, l_dn))
            else:
                self.live = (same(lambda p: self.half(p, 0), up, to_z_up, l_up),
                             same(lambda p: self.half(p, 1), dn, to_z_dn, l_dn))

        def advance(self):
            for copy in self.live:
                copy.got()
            self.hop += 1
            if self.hop < 4:
                self.start()

    class YPiece:
        def __init__(self, zz):
            full = lambda p: a1.at[p, zz]
            self.zz = zz
            self.up = same(full, y, to_y_up, y_dn)
            self.dn = same(full, y, to_y_dn, y_up)

        def forward(self):
            lower = lambda p: a1.at[p, self.zz, pl.ds(0, KH)]
            upper = lambda p: a1.at[p, self.zz, pl.ds(KH, KH)]
            self.up.got()
            self.f0 = same(lower, y_dn, to_y_up, y_op)
            self.dn.got()
            self.f1 = same(upper, y_up, to_y_dn, y_op)

        def finish(self):
            self.f0.got()
            self.f1.got()

    class XGather:
        def __init__(self):
            whole = lambda p: xr.at[p]
            self.up = same(whole, row, to_x_up, x_dn * 2 + c)
            self.dn = same(whole, row, to_x_dn, x_up * 2 + c)
            self.own = same(whole, row, to_core, x * 2 + oc)

        def forward(self):
            whole = lambda p: xr.at[p]
            self.up.got()
            self.f0 = same(lambda p: xr.at[p, halves[0]], x_dn * 2 + c, to_x_up, x_op * 2 + c)
            self.dn.got()
            self.f1 = same(lambda p: xr.at[p, halves[1]], x_up * 2 + c, to_x_dn, x_op * 2 + c)
            self.c0 = same(whole, x_dn * 2 + c, to_core, x_dn * 2 + oc)
            self.c1 = same(whole, x_up * 2 + c, to_core, x_up * 2 + oc)

        def finish(self):
            self.f0.got()
            self.f1.got()
            self.c2 = same(lambda p: xr.at[p], x_op * 2 + c, to_core, x_op * 2 + oc)

        def close(self):
            for copy in (self.own, self.c0, self.c1, self.c2):
                copy.got()

    class Spread:
        def __init__(self, k):
            self.k = k
            lo, hi = self.part(0), self.part(1)
            self.u0 = same(lo, x, to_x_up, x_dn)
            self.d1 = same(hi, x, to_x_dn, x_up)
            self.u1 = same(hi, x, to_x_up, x_dn)
            self.d0 = same(lo, x, to_x_dn, x_up)
            self.turn(x, 0)
            self.turn(x, 1)

        def part(self, h):
            return lambda p: xm.at[self.k, p, halves[h]]

        def turn(self, xx, h):
            k = self.k
            behind = (y + NY - xx) % NY
            i = len(sent)

            def copy():
                return pltpu.make_async_remote_copy(
                    src_ref=xm.at[k, xx, halves[h]], dst_ref=sb.at[k, c, y, halves[h]], send_sem=send.at[i],
                    recv_sem=arrive.at[k, behind * 2 + h], device_id=(row, xx * NZ + z), device_id_type=MESH)

            sent.append((copy(), behind != 0))

            @pl.when(behind != 0)
            def _():
                copy().start()

        def hop1(self):
            lo, hi = self.part(0), self.part(1)
            self.u0.got()
            self.f0 = same(lo, x_dn, to_x_up, x_op)
            self.turn(x_dn, 0)
            self.d1.got()
            self.f1 = same(hi, x_up, to_x_dn, x_op)
            self.turn(x_up, 1)
            self.u1.got()
            self.turn(x_dn, 1)
            self.d0.got()
            self.turn(x_up, 0)

        def hop2(self):
            k = self.k
            self.f0.got()
            self.turn(x_op, 0)
            self.f1.got()
            self.turn(x_op, 1)
            self.cores = [Copy(xm.at[k, y], sb.at[k, c, y], to_core, sb.at[k, oc, y])]

        def arrived(self):
            k = self.k
            for behind, to in ((1, to_y_up), (3, to_y_dn), (2, to_y_op)):
                src = (y + behind) % NY
                for h in range(2):
                    land = sb.at[k, c, src, halves[h]]
                    pltpu.make_async_remote_copy(
                        src_ref=land, dst_ref=land, send_sem=send.at[0], recv_sem=arrive.at[k, behind * 2 + h],
                        device_id=to, device_id_type=MESH).wait_recv()
                self.cores.append(same(lambda p: sb.at[k, p, src], c, to_core, oc))
            self.keep(c, y, xm[k, y])
            for behind in (1, 3, 2):
                src = (y + behind) % NY
                self.keep(c, src, sb[k, c, src])

        def keep(self, cc, src, value):
            hi, lo = split(value)
            sh[self.k, cc, 0, src] = hi
            sh[self.k, cc, 1, src] = lo

        def finish(self):
            for copy in self.cores:
                copy.got()
            for src in range(NY):
                self.keep(oc, src, sb[self.k, oc, src])

    def solve():
        total = jnp.zeros((TD, MD), F32)
        for r in range(2 * NX):
            hi, lo = split(xr[r])
            w = a1[r // 2, (r % 2) * 4:(r % 2) * 4 + 4].reshape(MD, MD)
            total = total + dot3(hi, lo, w)
        return total

    def partial(k, weight):
        total = jnp.zeros((NY * TD, MD), F32)
        for cc in range(2):
            hi = sh[k, cc, 0].reshape(NY * TD, MD)
            lo = sh[k, cc, 1].reshape(NY * TD, MD)
            total = total + dot3(hi, lo, weight(cc).reshape(MD, MD))
        return total.reshape(NY, TD, MD)

    def factor(i):
        return lambda cc: az[i, 4 * cc:4 * cc + 4]

    def panel(j, k):
        return lambda cc: pt[j, k, 4 * cc:4 * cc + 4]

    class YSum:
        def __init__(self, j):
            self.j = j
            self.a0 = Copy(part.at[j, y_op, halves[0]], r1.at[j, 0], to_y_up, r1.at[j, 0])
            self.a1 = Copy(part.at[j, y_op, halves[1]], r1.at[j, 1], to_y_dn, r1.at[j, 1])

        def forward(self):
            j = self.j
            self.a0.got()
            part[j, y_up, halves[0]] = part[j, y_up, halves[0]] + r1[j, 0]
            self.b0 = Copy(part.at[j, y_up], r2.at[j, 0], to_y_up, r2.at[j, 0])
            self.a1.got()
            part[j, y_dn, halves[1]] = part[j, y_dn, halves[1]] + r1[j, 1]
            self.b1 = Copy(part.at[j, y_dn], r2.at[j, 1], to_y_dn, r2.at[j, 1])

        def total(self):
            j = self.j
            self.b0.got()
            self.b1.got()
            return part[j, y] + (r2[j, 0] + r2[j, 1])

        def store(self):
            rows = pl.ds(self.j * MD, MD)
            trail[rows] = rhs_v[rows] - self.total().T

    local = []

    def bring(src, dst):
        copy = pltpu.make_async_copy(src, dst, loc.at[len(local)])
        local.append(copy)
        copy.start()

    bring(top_h, top_v)
    bring(inv_h.at[0], az.at[0, z])
    bring(cpl_h, az.at[1, z])
    bring(inv_h.at[1], a1.at[y, z])
    for j in range(CHUNKS):
        bring(pan_h.at[:, :, pl.ds(j * MD, MD)], pt.at[j, :, z])
    bring(rhs_h, rhs_v)

    barrier = pltpu.get_barrier_semaphore()
    peers = (to_x_up, to_x_dn, to_y_up, to_y_dn, to_y_op, to_z_up, to_z_dn, to_core)
    for peer in peers:
        pl.semaphore_signal(barrier, inc=1, device_id=peer, device_id_type=MESH)
    local[0].wait()
    xm[0, x] = top_v[0].T
    for copy in local[1:4]:
        copy.wait()
    pl.semaphore_wait(barrier, len(peers))

    spread0 = Spread(0)
    ring0 = ZRing(lambda p: az.at[0, p], lambda p, h: az.at[0, p, pl.ds(h * KH, KH)])
    ring1 = ZRing(lambda p: az.at[1, p], lambda p, h: az.at[1, p, pl.ds(h * KH, KH)])
    ring2 = ZRing(lambda p: a1.at[y, p], lambda p, h: a1.at[y, p, pl.ds(h * KH, KH)])
    rings = [ZRing(lambda p, j=j: pt.at[j, :, p], lambda p, h, j=j: pt.at[j, :, p, pl.ds(h * KH, KH)])
             for j in range(CHUNKS)]

    def at_z(d):
        return (z + NZ + d) % NZ

    ring0.start()
    ring1.start()
    ring2.start()
    pieces = [YPiece(z)]
    spread0.hop1()
    ring0.advance()
    ring1.advance()
    ring2.advance()
    pieces += [YPiece(at_z(-1))]
    spread0.hop2()
    ring0.advance()
    ring1.advance()
    ring2.advance()
    pieces += [YPiece(at_z(1))]
    spread0.arrived()
    ring0.advance()
    ring1.advance()
    ring2.advance()
    for copy in local[4:]:
        copy.wait()
    rings[0].start()
    rings[1].start()
    spread0.finish()
    ring0.advance()

    part[4] = partial(0, factor(0))
    sum4 = YSum(4)
    for piece in pieces:
        piece.forward()
    ring1.advance()
    ring2.advance()
    sum4.forward()
    pieces += [YPiece(at_z(d)) for d in (-2, 2)]
    rings[0].advance()
    first = sum4.total()
    xm[1, x] = first
    spread1 = Spread(1)
    solved[0] = first.T
    rings[1].advance()
    pieces[3].forward()
    pieces[4].forward()
    spread1.hop1()
    rings[0].advance()
    spread1.hop2()
    rings[1].advance()
    spread1.arrived()
    rings[0].advance()
    spread1.finish()

    part[5] = partial(1, factor(1))
    sum5 = YSum(5)
    pieces += [YPiece(at_z(d)) for d in (-3, 3, 4)]
    rings[1].advance()
    sum5.forward()
    for piece in pieces[5:]:
        piece.forward()
    rings[0].advance()
    rings[2].start()
    rings[1].advance()
    rings[3].start()
    reduced = top_v[1].T - sum5.total()
    xr[row] = reduced
    gather = XGather()
    for j in (0, 1):
        part[j] = partial(1, panel(j, 0))
    gather.forward()
    rings[2].advance()
    gather.finish()
    for piece in pieces:
        piece.finish()
    rings[3].advance()
    gather.close()
    second = solve()
    xm[2, x] = second
    spread2 = Spread(2)
    solved[1] = second.T
    rings[2].advance()
    spread2.hop1()
    rings[3].advance()
    spread2.hop2()
    rings[2].advance()
    rings[3].advance()
    spread2.arrived()
    rings[2].advance()
    spread2.finish()
    sums = []
    for j in (0, 1):
        part[j] = part[j] + partial(2, panel(j, 1))
        sums.append(YSum(j))
    rings[3].advance()
    sums[0].forward()
    part[2] = partial(1, panel(2, 0)) + partial(2, panel(2, 1))
    sums.append(YSum(2))
    sums[1].forward()
    part[3] = partial(1, panel(3, 0)) + partial(2, panel(3, 1))
    sums.append(YSum(3))
    sums[2].forward()
    sums[3].forward()
    for s in sums:
        s.store()
    for copy, when in sent:
        if when is None:
            copy.wait_send()
        else:
            pl.when(when)(copy.wait_send)


def body(inv_diag, coupling, top_rhs, panel, rhs):
    hbm = pl.BlockSpec(memory_space=pltpu.HBM)
    vmem = pl.BlockSpec(memory_space=pltpu.VMEM)
    solved, trailing = pl.pallas_call(
        kernel,
        out_shape=(jax.ShapeDtypeStruct((2, MD, TD), F32), jax.ShapeDtypeStruct((CHUNKS * MD, TD), F32)),
        in_specs=[hbm] * 5,
        out_specs=(vmem, vmem),
        scratch_shapes=[
            pltpu.VMEM((2, NZ, KD, MD), F32),
            pltpu.VMEM((NY, NZ, KD, MD), F32),
            pltpu.VMEM((CHUNKS, 2, NZ, KD, MD), F32),
            pltpu.VMEM((3, NX, TD, MD), F32),
            pltpu.VMEM((3, 2, NY, TD, MD), F32),
            pltpu.VMEM((3, 2, 2, NY, TD, MD), BF16),
            pltpu.VMEM((2 * NX, TD, MD), F32),
            pltpu.VMEM((CHUNKS + 2, NY, TD, MD), F32),
            pltpu.VMEM((CHUNKS + 2, 2, TH, MD), F32),
            pltpu.VMEM((CHUNKS + 2, 2, TD, MD), F32),
            pltpu.VMEM((2, MD, TD), F32),
            pltpu.VMEM((CHUNKS * MD, TD), F32),
            pltpu.SemaphoreType.DMA((N_COPIES,)),
            pltpu.SemaphoreType.DMA((N_COPIES,)),
            pltpu.SemaphoreType.DMA((3, 2 * NY)),
            pltpu.SemaphoreType.DMA((16,)),
        ],
        compiler_params=pltpu.CompilerParams(
            collective_id=0, has_side_effects=True, vmem_limit_bytes=60 * 1024 * 1024),
    )(jnp.swapaxes(inv_diag, 1, 2), coupling.T, top_rhs, jnp.swapaxes(panel, 1, 2), rhs)
    return solved, trailing


def solution(mesh):
    in_specs = (
        P(None, "row", "col"),
        P("row", "col"),
        P(None, "row", "col"),
        P(None, "row", "col"),
        P("row", "col"),
    )
    out_specs = (P(None, "row", "col"), P("row", "col"))
    return jax.shard_map(body, mesh=mesh, in_specs=in_specs, out_specs=out_specs, check_vma=False)
```

time: 525 us -> 118 us (0.22)
  waiting for transfers between devices: 472 us -> 0 us
  Pallas kernels: 0 us -> 115 us
  matrix products: 31.8 us -> 0 us
  between operations: 14.2 us -> 0.65 us
    all_gather x8 -> x0, waiting for transfers between devices: 470 us -> none  [the longest x1 141 us: body(): lax.all_gather(panel, 'col', axis=2, tiled=True)]
    pallas_call x0 -> x1, Pallas kernels: none -> 115 us  [body(): pl.pallas_call(kernel, out_shape=(jax.ShapeDtypeStruct((2, MD, TD), F32),...]
    dot_general x4 -> x0, matrix products: 31.8 us -> none  [the longest x3 17.9 us: product(): jnp.dot(left, right, precision=lax.Precision.HIGHEST, preferred_element_t...]
  transfers between devices with their start and end apart: 8 -> 0, of which waited for: 8 -> 0; matrix products, arithmetic and copies ran while one was open for 3% -> 0% of each run, Pallas kernels for 0% -> 0%
where the time goes in v2:
time: 118 us
  Pallas kernels  115 us (97%)
  local copies, waits for them, and re-layouts  2.52 us (2%)
    pallas_call x1, Pallas kernels, body(): pl.pallas_call(kernel, out_shape=(jax.ShapeDtypeStruct((2, MD, TD), F32),...  115 us
    unnamed x4, local copies, waits for them, and re-layouts  2.52 us

profile of v2, /device:TPU:1, one launch (start us, length us, event | category | flops | bytes accessed | tf_op | source)
XLA Modules:
  0.0 117.7 jit_solution(11558395329409739570)
XLA Ops:
  0.6 114.5 %shard_map.68 = (f32[2,256,128]{2,1,0:T(8,128)}, f32[1024,128]{1,0:T(8,128)}) custom-call(f32[2,64,256]{2,1,0:T(8,128)} %bitcast.4, f32[64,256]{1,0:T(8,128)} %bitcast.5, f32[2,256,128]{2,1,0:T(8,128)} %top_h.1, f32[2,64,1024]{2,1,0:T(8,128)} %bitcast.3, f32[1024,128]{1,0:T(8,128)} %rhs_h.1), custom_call_target="tpu_custom_call" | custom-call | tf_op jit(solution)/shard_map/pallas_call | solution.py:399
  115.2 0.0 copy-start
  115.2 1.7 %copy.9 = f32[2,256,128]{2,1,0:T(8,128)} copy(f32[2,256,128]{2,1,0:T(8,128)} %get-tuple-element.4) | data formatting | bytes 524288
  116.9 0.0 copy-done
  116.9 0.8 copy.10
Async XLA Ops:
  115.2 1.7 %copy-start = (f32[1024,128]{1,0:T(8,128)S(1)}, f32[1024,128]{1,0:T(8,128)}, u32[]{:S(2)}) copy-start(f32[1024,128]{1,0:T(8,128)} %get-tuple-element.5) | copy-start | bytes 1572868

commit v3 on v0

v3 whole, which is shorter than its diff:
```python
import jax
import jax.numpy as jnp
from jax import lax
from jax.experimental import pallas as pl
from jax.experimental.pallas import tpu as pltpu
from jax.sharding import PartitionSpec as P

MESH = pl.DeviceIdType.MESH
F32 = jnp.float32
BF16 = jnp.bfloat16
NX, NY, NZ = 4, 4, 8
KD, MD, TD = 64, 256, 128
KH = KD // 2
CHUNKS = 4
N_COPIES = 240


def split(v):
    hi = v.astype(BF16)
    lo = (v - hi.astype(F32)).astype(BF16)
    return hi, lo


def dot(a, b):
    return jnp.dot(a, b, preferred_element_type=F32)


def dot3(hi, lo, w):
    wh, wl = split(w)
    return dot(hi, wh) + (dot(lo, wh) + dot(hi, wl))


def kernel(inv_h, cpl_h, top_h, pan_h, rhs_h, solved, trail,
           az, pt, xs, sb, sh, part, rs, top_v, rhs_v, send, recv, arrive, loc):
    row, col = lax.axis_index("row"), lax.axis_index("col")
    x, c = row // 2, row % 2
    y, z = col // NZ, col % NZ
    oc = 1 - c
    x_up, x_dn, x_op = (x + 1) % NX, (x + NX - 1) % NX, (x + 2) % NX
    y_up, y_dn, y_op = (y + 1) % NY, (y + NY - 1) % NY, (y + 2) % NY
    to_x_up, to_x_dn = (x_up * 2 + c, col), (x_dn * 2 + c, col)
    to_y_up, to_y_dn, to_y_op = (row, y_up * NZ + z), (row, y_dn * NZ + z), (row, y_op * NZ + z)
    to_z_up, to_z_dn = (row, y * NZ + (z + 1) % NZ), (row, y * NZ + (z + NZ - 1) % NZ)
    to_x_op = (x_op * 2 + c, col)
    to_core = (x * 2 + oc, col)

    halves = (pl.ds(0, TD // 2), pl.ds(TD // 2, TD // 2))

    def at_z(d):
        return (z + NZ + d) % NZ

    sent = []

    class Copy:
        def __init__(self, src, dst, to, land):
            i = len(sent)
            self.out = pltpu.make_async_remote_copy(
                src_ref=src, dst_ref=dst, send_sem=send.at[i], recv_sem=recv.at[i], device_id=to, device_id_type=MESH)
            self.into = pltpu.make_async_remote_copy(
                src_ref=land, dst_ref=land, send_sem=send.at[i], recv_sem=recv.at[i], device_id=to, device_id_type=MESH)
            sent.append((self.out, None))
            self.out.start()

        def got(self):
            self.into.wait_recv()

    def same(view, at, to, land):
        return Copy(view(at), view(at), to, view(land))

    class ZRing:
        def __init__(self, full, half):
            self.full, self.half, self.hop = full, half, 0

        def start(self):
            s = self.hop
            up, dn = (z + NZ - s) % NZ, (z + s) % NZ
            l_up, l_dn = (z + NZ - 1 - s) % NZ, (z + 1 + s) % NZ
            if s < 3:
                self.live = (same(self.full, up, to_z_up, l_up), same(self.full, dn, to_z_dn, l_dn))
            else:
                self.live = (same(lambda p: self.half(p, 0), up, to_z_up, l_up),
                             same(lambda p: self.half(p, 1), dn, to_z_dn, l_dn))

        def advance(self):
            for copy in self.live:
                copy.got()
            self.hop += 1
            if self.hop < 4:
                self.start()

    class ZPair:
        def __init__(self, full, half):
            self.full, self.half = full, half
            self.near = [same(full, z, (row, y * NZ + at_z(d)), at_z(-d)) for d in (2, -2, 1, -1)]

        def forward(self):
            far_up, far_dn = (row, y * NZ + at_z(2)), (row, y * NZ + at_z(-2))
            for copy in self.near[2:]:
                copy.got()
            self.far = [same(self.full, at_z(-1), far_up, at_z(-3)), same(self.full, at_z(1), far_dn, at_z(3))]
            for copy in self.near[:2]:
                copy.got()
            self.far += [same(lambda p: self.half(p, 0), at_z(-2), far_up, at_z(4)),
                         same(lambda p: self.half(p, 1), at_z(2), far_dn, at_z(4))]

        def finish(self):
            for copy in self.far:
                copy.got()

    class Inbox:
        def __init__(self, k):
            self.k, self.cores = k, []

        def post(self, src, to, behind, when=None):
            k, i = self.k, len(sent)

            def copy():
                return pltpu.make_async_remote_copy(
                    src_ref=src, dst_ref=sb.at[k, c, y], send_sem=send.at[i], recv_sem=arrive.at[k, behind],
                    device_id=to, device_id_type=MESH)

            sent.append((copy(), when))
            if when is None:
                copy().start()
            else:
                @pl.when(when)
                def _():
                    copy().start()

        def take(self, behind, when=None):
            k = self.k
            src = (y + behind) % NY
            land = sb.at[k, c, src]

            def wait():
                pltpu.make_async_remote_copy(
                    src_ref=land, dst_ref=land, send_sem=send.at[0], recv_sem=arrive.at[k, behind],
                    device_id=to_core, device_id_type=MESH).wait_recv()

            if when is None:
                wait()
            else:
                pl.when(when)(wait)
            self.share(src)

        def share(self, src):
            self.cores.append(same(lambda p: sb.at[self.k, p, src], c, to_core, oc))

        def keep(self, cc):
            for src in range(NY):
                hi, lo = split(sb[self.k, cc, src])
                sh[self.k, cc, 0, src] = hi
                sh[self.k, cc, 1, src] = lo

        def finish(self):
            self.keep(c)
            for copy in self.cores:
                copy.got()
            self.keep(oc)

    class Spread(Inbox):
        def __init__(self, k):
            super().__init__(k)
            behind = (y + NY - x) % NY
            for xx in (x_op, x_up, x_dn):
                self.post(xs.at[k], (xx * 2 + c, x * NZ + z), behind)
            self.post(xs.at[k], (row, x * NZ + z), behind, x != y)

            @pl.when(x == y)
            def _():
                sb[k, c, y] = xs[k]

        def arrived(self):
            for behind in (1, 3, 2):
                self.take(behind)
            self.take(0, x != y)

    def partial(k, weight):
        total = jnp.zeros((NY * TD, MD), F32)
        for cc in range(2):
            hi = sh[k, cc, 0].reshape(NY * TD, MD)
            lo = sh[k, cc, 1].reshape(NY * TD, MD)
            total = total + dot3(hi, lo, weight(cc).reshape(MD, MD))
        return total.reshape(NY, TD, MD)

    def panel(j, k):
        return lambda cc: pt[j, k, 4 * cc:4 * cc + 4]

    class YSum:
        def __init__(self, j):
            self.j = j
            self.live = [Copy(part.at[j, yy], rs.at[j, n], to, rs.at[j, n]) for n, (yy, to) in
                         enumerate(((y_op, to_y_op), (y_up, to_y_up), (y_dn, to_y_dn)))]

        def total(self):
            j = self.j
            for copy in self.live:
                copy.got()
            return (part[j, y] + rs[j, 0]) + (rs[j, 1] + rs[j, 2])

    class YRelay:
        def __init__(self, j):
            self.j = j
            self.a0 = Copy(part.at[j, y_op, halves[0]], rs.at[j, 2, halves[0]], to_y_up, rs.at[j, 2, halves[0]])
            self.a1 = Copy(part.at[j, y_op, halves[1]], rs.at[j, 2, halves[1]], to_y_dn, rs.at[j, 2, halves[1]])
            self.live = [self.send(0, y_up, 1, to_y_up), self.send(1, y_dn, 0, to_y_dn)]

        def send(self, way, to, h, device):
            land = rs.at[self.j, way, halves[h]]
            return Copy(part.at[self.j, to, halves[h]], land, device, land)

        def forward(self):
            j = self.j
            self.a0.got()
            part[j, y_up, halves[0]] = part[j, y_up, halves[0]] + rs[j, 2, halves[0]]
            self.live.append(self.send(0, y_up, 0, to_y_up))
            self.a1.got()
            part[j, y_dn, halves[1]] = part[j, y_dn, halves[1]] + rs[j, 2, halves[1]]
            self.live.append(self.send(1, y_dn, 1, to_y_dn))

        def store(self):
            j = self.j
            for copy in self.live:
                copy.got()
            rows = pl.ds(j * MD, MD)
            trail[rows] = rhs_v[rows] - (part[j, y] + (rs[j, 0] + rs[j, 1])).T

    local = []

    def bring(src, dst):
        copy = pltpu.make_async_copy(src, dst, loc.at[len(local)])
        local.append(copy)
        copy.start()

    bring(top_h, top_v)
    bring(inv_h.at[0], az.at[0, z])
    bring(cpl_h, az.at[1, z])
    bring(inv_h.at[1], az.at[2, z])
    for j in range(CHUNKS):
        bring(pan_h.at[:, :, pl.ds(j * MD, MD)], pt.at[j, :, z])
    bring(rhs_h, rhs_v)

    barrier = pltpu.get_barrier_semaphore()
    peers = [(((x + dx) % NX) * 2 + c, ((y + dy) % NY) * NZ + z) for dx in range(NX) for dy in range(NY) if dx or dy]
    peers += [(row, y * NZ + at_z(d)) for d in range(1, NZ)] + [to_core]
    for peer in peers:
        pl.semaphore_signal(barrier, inc=1, device_id=peer, device_id_type=MESH)
    local[0].wait()
    xs[0] = top_v[0].T
    for copy in local[1:4]:
        copy.wait()
    pl.semaphore_wait(barrier, len(peers))

    views = lambda i: (lambda p: az.at[i, p], lambda p, h: az.at[i, p, pl.ds(h * KH, KH)])
    rings = [ZRing(lambda p, j=j: pt.at[j, :, p], lambda p, h, j=j: pt.at[j, :, p, pl.ds(h * KH, KH)])
             for j in range(CHUNKS)]
    factor = lambda i: lambda cc: az[i, 4 * cc:4 * cc + 4]

    spread0 = Spread(0)
    pair0 = ZPair(*views(0))
    ring_c, ring_a = ZRing(*views(1)), ZRing(*views(2))
    ring_c.start()
    pair0.forward()
    ring_c.advance()
    ring_a.start()
    for copy in local[4:]:
        copy.wait()
    spread0.arrived()
    spread0.finish()
    ring_c.advance()
    pair0.finish()
    part[4] = partial(0, factor(0))
    sum4 = YSum(4)
    ring_a.advance()
    rings[0].start()
    ring_c.advance()
    rings[1].start()
    ring_a.advance()
    first = sum4.total()
    xs[1] = first
    spread1 = Spread(1)
    solved[0] = first.T
    ring_c.advance()
    rings[0].advance()
    ring_a.advance()
    rings[1].advance()
    spread1.arrived()
    ring_a.advance()
    spread1.finish()
    part[5] = partial(1, factor(1))
    sum5 = YSum(5)
    rings[0].advance()
    rings[1].advance()
    reduced = top_v[1].T - sum5.total()
    xs[2] = reduced
    spread2 = Spread(2)
    rings[0].advance()
    rings[1].advance()
    spread2.arrived()
    rings[2].start()
    rings[3].start()
    spread2.finish()
    part[6] = partial(2, factor(2))
    sum6 = YSum(6)
    rings[0].advance()
    part[0] = partial(1, panel(0, 0))
    rings[1].advance()
    part[1] = partial(1, panel(1, 0))
    second = sum6.total()
    xs[3] = second
    spread3 = Spread(3)
    solved[1] = second.T
    rings[2].advance()
    rings[3].advance()
    spread3.arrived()
    rings[2].advance()
    rings[3].advance()
    spread3.finish()
    sums = []
    part[0] = part[0] + partial(3, panel(0, 1))
    sums.append(YRelay(0))
    part[1] = part[1] + partial(3, panel(1, 1))
    sums.append(YRelay(1))
    rings[2].advance()
    rings[3].advance()
    sums[0].forward()
    sums[1].forward()
    rings[2].advance()
    part[2] = partial(1, panel(2, 0)) + partial(3, panel(2, 1))
    sums.append(YRelay(2))
    rings[3].advance()
    part[3] = partial(1, panel(3, 0)) + partial(3, panel(3, 1))
    sums.append(YRelay(3))
    sums[2].forward()
    sums[3].forward()
    for s in sums:
        s.store()
    for copy, when in sent:
        if when is None:
            copy.wait_send()
        else:
            pl.when(when)(copy.wait_send)


def body(inv_diag, coupling, top_rhs, panel, rhs):
    hbm = pl.BlockSpec(memory_space=pltpu.HBM)
    vmem = pl.BlockSpec(memory_space=pltpu.VMEM)
    solved, trailing = pl.pallas_call(
        kernel,
        out_shape=(jax.ShapeDtypeStruct((2, MD, TD), F32), jax.ShapeDtypeStruct((CHUNKS * MD, TD), F32)),
        in_specs=[hbm] * 5,
        out_specs=(vmem, vmem),
        scratch_shapes=[
            pltpu.VMEM((3, NZ, KD, MD), F32),
            pltpu.VMEM((CHUNKS, 2, NZ, KD, MD), F32),
            pltpu.VMEM((4, TD, MD), F32),
            pltpu.VMEM((4, 2, NY, TD, MD), F32),
            pltpu.VMEM((4, 2, 2, NY, TD, MD), BF16),
            pltpu.VMEM((CHUNKS + 3, NY, TD, MD), F32),
            pltpu.VMEM((CHUNKS + 3, NY - 1, TD, MD), F32),
            pltpu.VMEM((2, MD, TD), F32),
            pltpu.VMEM((CHUNKS * MD, TD), F32),
            pltpu.SemaphoreType.DMA((N_COPIES,)),
            pltpu.SemaphoreType.DMA((N_COPIES,)),
            pltpu.SemaphoreType.DMA((4, NY)),
            pltpu.SemaphoreType.DMA((16,)),
        ],
        compiler_params=pltpu.CompilerParams(
            collective_id=0, has_side_effects=True, vmem_limit_bytes=62 * 1024 * 1024),
    )(jnp.swapaxes(inv_diag, 1, 2), coupling.T, top_rhs, jnp.swapaxes(panel, 1, 2), rhs)
    return solved, trailing


def solution(mesh):
    in_specs = (
        P(None, "row", "col"),
        P("row", "col"),
        P(None, "row", "col"),
        P(None, "row", "col"),
        P("row", "col"),
    )
    out_specs = (P(None, "row", "col"), P("row", "col"))
    return jax.shard_map(body, mesh=mesh, in_specs=in_specs, out_specs=out_specs, check_vma=False)
```

time: 525 us -> 114 us (0.22)
  the two profiles are of different devices: /device:TPU:1 before, /device:TPU:12 now
where the time goes in v3:
time: 114 us; the launch traced here: 113 us
  Pallas kernels  110 us (96%)
  local copies, waits for them, and re-layouts  2.52 us (2%)
    pallas_call x1, Pallas kernels, body(): pl.pallas_call(kernel, out_shape=(jax.ShapeDtypeStruct((2, MD, TD), F32),...  110 us
    unnamed x4, local copies, waits for them, and re-layouts  2.52 us

profile of v3, /device:TPU:12, one launch (start us, length us, event | category | flops | bytes accessed | tf_op | source)
XLA Modules:
  0.0 113.4 jit_solution(16469710516669123758)
XLA Ops:
  0.6 110.2 %shard_map.68 = (f32[2,256,128]{2,1,0:T(8,128)}, f32[1024,128]{1,0:T(8,128)}) custom-call(f32[2,64,256]{2,1,0:T(8,128)} %bitcast.4, f32[64,256]{1,0:T(8,128)} %bitcast.5, f32[2,256,128]{2,1,0:T(8,128)} %top_h.1, f32[2,64,1024]{2,1,0:T(8,128)} %bitcast.3, f32[1024,128]{1,0:T(8,128)} %rhs_h.1), custom_call_target="tpu_custom_call" | custom-call | tf_op jit(solution)/shard_map/pallas_call | solution.py:348
  110.9 0.0 copy-start
  110.9 1.7 %copy.9 = f32[2,256,128]{2,1,0:T(8,128)} copy(f32[2,256,128]{2,1,0:T(8,128)} %get-tuple-element.4) | data formatting | bytes 524288
  112.6 0.0 copy-done
  112.6 0.8 copy.10
Async XLA Ops:
  110.9 1.7 %copy-start = (f32[1024,128]{1,0:T(8,128)S(1)}, f32[1024,128]{1,0:T(8,128)}, u32[]{:S(2)}) copy-start(f32[1024,128]{1,0:T(8,128)} %get-tuple-element.5) | copy-start | bytes 1572868

commit v4 on v0

v4 whole, which is shorter than its diff:
```python
import jax
import jax.numpy as jnp
from jax import lax
from jax.experimental import pallas as pl
from jax.experimental.pallas import tpu as pltpu
from jax.sharding import PartitionSpec as P

MESH = pl.DeviceIdType.MESH
F32 = jnp.float32
BF16 = jnp.bfloat16
NX, NY, NZ = 4, 4, 8
KD, MD, TD = 64, 256, 128
KH = KD // 2
CHUNKS = 4
N_SEND, N_RECV, N_LOCAL = 29, 46, 9


def split(v):
    hi = v.astype(BF16)
    lo = (v - hi.astype(F32)).astype(BF16)
    return hi, lo


def dot(a, b):
    return jnp.dot(a, b, preferred_element_type=F32)


def dot3(hi, lo, w):
    wh, wl = split(w)
    return dot(hi, wh) + (dot(lo, wh) + dot(hi, wl))


def kernel(inv_h, cpl_h, top_h, pan_h, rhs_h, solved, trail,
           az, pt, xs, sb, sh, cb, ch, xc, part, rs, wp, wr, top_v, rhs_v, send, recv, arrive, loc):
    row, col = lax.axis_index("row"), lax.axis_index("col")
    x, c = row // 2, row % 2
    y, z = col // NZ, col % NZ
    oc = 1 - c
    x_up, x_dn, x_op = (x + 1) % NX, (x + NX - 1) % NX, (x + 2) % NX
    y_up, y_dn, y_op = (y + 1) % NY, (y + NY - 1) % NY, (y + 2) % NY
    to_x_up, to_x_dn = (x_up * 2 + c, col), (x_dn * 2 + c, col)
    to_y_up, to_y_dn, to_y_op = (row, y_up * NZ + z), (row, y_dn * NZ + z), (row, y_op * NZ + z)
    to_z_up, to_z_dn = (row, y * NZ + (z + 1) % NZ), (row, y * NZ + (z + NZ - 1) % NZ)
    to_x_op = (x_op * 2 + c, col)
    to_core = (x * 2 + oc, col)

    halves = (pl.ds(0, TD // 2), pl.ds(TD // 2, TD // 2))

    def at_z(d):
        return (z + NZ + d) % NZ

    used = {"send": 0, "recv": 0}
    drains = []

    def fresh(kind):
        used[kind] += 1
        return used[kind] - 1

    def group(ref, when=None):
        s = fresh("send")
        drains.append((ref, s, when))
        return s

    def remote(src, dst, to, s, sem):
        return pltpu.make_async_remote_copy(
            src_ref=src, dst_ref=dst, send_sem=send.at[s], recv_sem=sem, device_id=to, device_id_type=MESH)

    def push(src, dst, to, s, r):
        remote(src, dst, to, s, recv.at[r]).start()

    def move(view, at, to, s, r):
        push(view(at), view(at), to, s, r)

    def got(ref, r):
        remote(ref, ref, to_core, 0, recv.at[r]).wait_recv()

    class ZRing:
        def __init__(self, full, half, run):
            self.full, self.half, self.run, self.hop, self.s = full, half, run, 0, group(run(7))

        def start(self):
            s = self.hop
            up, dn = (z + NZ - s) % NZ, (z + s) % NZ
            self.r = fresh("recv")
            for at, to, h in ((up, to_z_up, 0), (dn, to_z_dn, 1)):
                move(self.full if s < 3 else lambda p: self.half(p, h), at, to, self.s, self.r)

        def advance(self):
            got(self.run(2 if self.hop < 3 else 1), self.r)
            self.hop += 1
            if self.hop < 4:
                self.start()

    class ZPair:
        def __init__(self, full, half, run):
            self.full, self.half, self.run, self.s = full, half, run, group(run(7))
            self.r = [fresh("recv") for _ in range(3)]
            for d in (2, -2, 1, -1):
                move(full, z, (row, y * NZ + at_z(d)), self.s, self.r[abs(d) - 1])

        def forward(self):
            far_up, far_dn = (row, y * NZ + at_z(2)), (row, y * NZ + at_z(-2))
            got(self.run(2), self.r[0])
            move(self.full, at_z(-1), far_up, self.s, self.r[2])
            move(self.full, at_z(1), far_dn, self.s, self.r[2])
            got(self.run(2), self.r[1])
            move(lambda p: self.half(p, 0), at_z(-2), far_up, self.s, self.r[2])
            move(lambda p: self.half(p, 1), at_z(2), far_dn, self.s, self.r[2])

        def finish(self):
            got(self.run(3), self.r[2])

    class Spread:
        def __init__(self, k, src, box, kept):
            self.k, self.box, self.kept = k, box, kept
            self.s, self.r = group(box.at[0]), fresh("recv")
            behind = (y + NY - x) % NY
            here = group(src, x != y)
            there = group(box.at[0, pl.ds(0, 3)])
            for xx in (x_op, x_up, x_dn):
                self.post(src, (xx * 2 + c, x * NZ + z), behind, there).start()

            @pl.when(x != y)
            def _():
                self.post(src, (row, x * NZ + z), behind, here).start()

            @pl.when(x == y)
            def _():
                box[c, y] = src[...]

        def post(self, src, to, behind, s):
            return remote(src, self.box.at[c, y], to, s, arrive.at[self.k, behind])

        def arrived(self):
            for behind in (1, 3, 2, 0):
                src = (y + behind) % NY
                land = self.box.at[c, src]

                def wait():
                    remote(land, land, to_core, 0, arrive.at[self.k, behind]).wait_recv()

                if behind:
                    wait()
                else:
                    pl.when(x != y)(wait)
                push(land, land, to_core, self.s, self.r)

        def keep(self, cc):
            for src in range(NY):
                hi, lo = split(self.box[cc, src])
                self.kept[cc, 0, src] = hi
                self.kept[cc, 1, src] = lo

        def finish(self):
            self.keep(c)
            got(self.box.at[0], self.r)
            self.keep(oc)

    def partial(kept, weight):
        rows = kept.shape[-2]
        total = jnp.zeros((NY * rows, MD), F32)
        for cc in range(2):
            hi = kept[cc, 0].reshape(NY * rows, MD)
            lo = kept[cc, 1].reshape(NY * rows, MD)
            total = total + dot3(hi, lo, weight(cc).reshape(MD, MD))
        return total.reshape(NY, rows, MD)

    def panel(j, k):
        return lambda cc: pt[j, k, 4 * cc:4 * cc + 4]

    class YSum:
        def __init__(self, mine, theirs):
            self.mine, self.theirs, self.r = mine, theirs, fresh("recv")
            s = group(theirs)
            for n, (yy, to) in enumerate(((y_op, to_y_op), (y_up, to_y_up), (y_dn, to_y_dn))):
                push(mine.at[yy], theirs.at[n], to, s, self.r)

        def total(self):
            got(self.theirs, self.r)
            return (self.mine[y] + self.theirs[0]) + (self.theirs[1] + self.theirs[2])

    class YRelay:
        def __init__(self, j):
            self.j, self.s = j, group(rs.at[j])
            self.r = [fresh("recv") for _ in range(3)]
            for h, to in enumerate((to_y_up, to_y_dn)):
                push(part.at[j, y_op, halves[h]], rs.at[j, 2, halves[h]], to, self.s, self.r[h])
            self.pass_on(0, y_up, 1, to_y_up)
            self.pass_on(1, y_dn, 0, to_y_dn)

        def pass_on(self, way, yy, h, to):
            push(part.at[self.j, yy, halves[h]], rs.at[self.j, way, halves[h]], to, self.s, self.r[2])

        def forward(self):
            j = self.j
            for h, yy, to in ((0, y_up, to_y_up), (1, y_dn, to_y_dn)):
                got(rs.at[j, 2, halves[h]], self.r[h])
                part[j, yy, halves[h]] = part[j, yy, halves[h]] + rs[j, 2, halves[h]]
                self.pass_on(h, yy, h, to)

        def store(self):
            j = self.j
            got(rs.at[j, pl.ds(0, 2)], self.r[2])
            rows = pl.ds(j * MD, MD)
            trail[rows] = rhs_v[rows] - (part[j, y] + (rs[j, 0] + rs[j, 1])).T

    local = []

    def bring(src, dst):
        copy = pltpu.make_async_copy(src, dst, loc.at[len(local)])
        local.append(copy)
        copy.start()

    bring(top_h, top_v)
    bring(inv_h.at[0], az.at[0, z])
    bring(cpl_h, xc)
    bring(inv_h.at[1], az.at[2, z])
    for j in range(CHUNKS):
        bring(pan_h.at[:, :, pl.ds(j * MD, MD)], pt.at[j, :, z])
    bring(rhs_h, rhs_v)

    barrier = pltpu.get_barrier_semaphore()
    peers = [(((x + dx) % NX) * 2 + c, ((y + dy) % NY) * NZ + z) for dx in range(NX) for dy in range(NY) if dx or dy]
    peers += [(row, y * NZ + at_z(d)) for d in range(1, NZ)] + [to_core]
    for peer in peers:
        pl.semaphore_signal(barrier, inc=1, device_id=peer, device_id_type=MESH)
    local[0].wait()
    xs[0] = top_v[0].T
    xs[2] = top_v[1].T
    for copy in local[1:4]:
        copy.wait()
    pl.semaphore_wait(barrier, len(peers))

    views = lambda i: (lambda p: az.at[i, p], lambda p, h: az.at[i, p, pl.ds(h * KH, KH)],
                       lambda n: az.at[i, pl.ds(0, n)])
    rings = [ZRing(lambda p, j=j: pt.at[j, :, p], lambda p, h, j=j: pt.at[j, :, p, pl.ds(h * KH, KH)],
                   lambda n, j=j: pt.at[j, :, pl.ds(0, n)]) for j in range(CHUNKS)]
    factor = lambda i: lambda cc: az[i, 4 * cc:4 * cc + 4]
    kept = lambda k: sh.at[k]
    spread = lambda k: Spread(k, xs.at[k], sb.at[k], sh.at[k])

    spread0 = spread(0)
    ring_a = ZRing(*views(2))
    ring_a.start()
    pair0 = ZPair(*views(0))
    spread_c = Spread(4, xc, cb, ch)
    spread2 = spread(2)
    pair0.forward()
    ring_a.advance()
    for copy in local[4:]:
        copy.wait()
    rings[0].start()
    spread0.arrived()
    spread_c.arrived()
    spread0.finish()
    ring_a.advance()
    rings[1].start()
    pair0.finish()
    part[4] = partial(kept(0), factor(0))
    sum_f = YSum(part.at[4], rs.at[4])
    spread_c.finish()
    spread2.arrived()
    ring_a.advance()
    spread2.finish()
    ring_a.advance()
    wp[...] = partial(ch, factor(2))
    sum_w = YSum(wp, wr)
    rings[0].advance()
    first = sum_f.total()
    xs[1] = first
    spread1 = spread(1)
    solved[0] = first.T
    part[5] = partial(kept(2), factor(2))
    az[1, z] = sum_w.total()
    pair_w = ZPair(*views(1))
    rings[1].advance()
    pair_w.forward()
    rings[2].start()
    rings[3].start()
    rings[0].advance()
    spread1.arrived()
    spread1.finish()
    rings[1].advance()
    pair_w.finish()
    part[5] = part[5] - partial(kept(1), factor(1))
    sum_s = YSum(part.at[5], rs.at[5])
    rings[2].advance()
    rings[3].advance()
    second = sum_s.total()
    xs[3] = second
    spread3 = spread(3)
    solved[1] = second.T
    rings[0].advance()
    rings[1].advance()
    rings[2].advance()
    rings[3].advance()
    rings[0].advance()
    part[0] = partial(kept(1), panel(0, 0))
    spread3.arrived()
    spread3.finish()
    sums = []
    part[0] = part[0] + partial(kept(3), panel(0, 1))
    sums.append(YRelay(0))
    rings[1].advance()
    part[1] = partial(kept(1), panel(1, 0)) + partial(kept(3), panel(1, 1))
    sums.append(YRelay(1))
    rings[2].advance()
    rings[3].advance()
    sums[0].forward()
    rings[2].advance()
    part[2] = partial(kept(1), panel(2, 0)) + partial(kept(3), panel(2, 1))
    sums.append(YRelay(2))
    sums[1].forward()
    rings[3].advance()
    part[3] = partial(kept(1), panel(3, 0)) + partial(kept(3), panel(3, 1))
    sums.append(YRelay(3))
    sums[2].forward()
    sums[3].forward()
    for s in sums:
        s.store()
    for ref, i, when in drains:
        wait = remote(ref, ref, to_core, i, recv.at[0]).wait_send
        if when is None:
            wait()
        else:
            pl.when(when)(wait)
    assert (used["send"], used["recv"], len(local)) == (N_SEND, N_RECV, N_LOCAL), used


def body(inv_diag, coupling, top_rhs, panel, rhs):
    hbm = pl.BlockSpec(memory_space=pltpu.HBM)
    vmem = pl.BlockSpec(memory_space=pltpu.VMEM)
    solved, trailing = pl.pallas_call(
        kernel,
        out_shape=(jax.ShapeDtypeStruct((2, MD, TD), F32), jax.ShapeDtypeStruct((CHUNKS * MD, TD), F32)),
        in_specs=[hbm] * 5,
        out_specs=(vmem, vmem),
        scratch_shapes=[
            pltpu.VMEM((3, NZ, KD, MD), F32),
            pltpu.VMEM((CHUNKS, 2, NZ, KD, MD), F32),
            pltpu.VMEM((4, TD, MD), F32),
            pltpu.VMEM((4, 2, NY, TD, MD), F32),
            pltpu.VMEM((4, 2, 2, NY, TD, MD), BF16),
            pltpu.VMEM((2, NY, KD, MD), F32),
            pltpu.VMEM((2, 2, NY, KD, MD), BF16),
            pltpu.VMEM((KD, MD), F32),
            pltpu.VMEM((CHUNKS + 2, NY, TD, MD), F32),
            pltpu.VMEM((CHUNKS + 2, NY - 1, TD, MD), F32),
            pltpu.VMEM((NY, KD, MD), F32),
            pltpu.VMEM((NY - 1, KD, MD), F32),
            pltpu.VMEM((2, MD, TD), F32),
            pltpu.VMEM((CHUNKS * MD, TD), F32),
            pltpu.SemaphoreType.DMA((N_SEND,)),
            pltpu.SemaphoreType.DMA((N_RECV,)),
            pltpu.SemaphoreType.DMA((5, NY)),
            pltpu.SemaphoreType.DMA((N_LOCAL,)),
        ],
        compiler_params=pltpu.CompilerParams(
            collective_id=0, has_side_effects=True, vmem_limit_bytes=62 * 1024 * 1024),
    )(jnp.swapaxes(inv_diag, 1, 2), coupling.T, top_rhs, jnp.swapaxes(panel, 1, 2), rhs)
    return solved, trailing


def solution(mesh):
    in_specs = (
        P(None, "row", "col"),
        P("row", "col"),
        P(None, "row", "col"),
        P(None, "row", "col"),
        P("row", "col"),
    )
    out_specs = (P(None, "row", "col"), P("row", "col"))
    return jax.shard_map(body, mesh=mesh, in_specs=in_specs, out_specs=out_specs, check_vma=False)
```

time: 525 us -> 101 us (0.19)
  waiting for transfers between devices: 472 us -> 0 us
  Pallas kernels: 0 us -> 97.2 us
  matrix products: 31.8 us -> 0 us
  between operations: 14.2 us -> 0.65 us
    all_gather x8 -> x0, waiting for transfers between devices: 470 us -> none  [the longest x1 141 us: body(): lax.all_gather(panel, 'col', axis=2, tiled=True)]
    pallas_call x0 -> x1, Pallas kernels: none -> 97.2 us  [body(): pl.pallas_call(kernel, out_shape=(jax.ShapeDtypeStruct((2, MD, TD), F32),...]
    dot_general x4 -> x0, matrix products: 31.8 us -> none  [the longest x3 17.9 us: product(): jnp.dot(left, right, precision=lax.Precision.HIGHEST, preferred_element_t...]
  transfers between devices with their start and end apart: 8 -> 0, of which waited for: 8 -> 0; matrix products, arithmetic and copies ran while one was open for 3% -> 0% of each run, Pallas kernels for 0% -> 0%
where the time goes in v4:
time: 101 us; the launch traced here: 100 us
  Pallas kernels  97.2 us (96%)
  local copies, waits for them, and re-layouts  2.52 us (2%)
    pallas_call x1, Pallas kernels, body(): pl.pallas_call(kernel, out_shape=(jax.ShapeDtypeStruct((2, MD, TD), F32),...  97.2 us
    unnamed x4, local copies, waits for them, and re-layouts  2.52 us

profile of v4, /device:TPU:1, one launch (start us, length us, event | category | flops | bytes accessed | tf_op | source)
XLA Modules:
  0.0 100.4 jit_solution(12028564508100399879)
XLA Ops:
  0.6 97.2 %shard_map.68 = (f32[2,256,128]{2,1,0:T(8,128)}, f32[1024,128]{1,0:T(8,128)}) custom-call(f32[2,64,256]{2,1,0:T(8,128)} %bitcast.4, f32[64,256]{1,0:T(8,128)} %bitcast.5, f32[2,256,128]{2,1,0:T(8,128)} %top_h.1, f32[2,64,1024]{2,1,0:T(8,128)} %bitcast.3, f32[1024,128]{1,0:T(8,128)} %rhs_h.1), custom_call_target="tpu_custom_call" | custom-call | tf_op jit(solution)/shard_map/pallas_call | solution.py:333
  97.9 0.0 copy-start
  97.9 1.7 %copy.9 = f32[2,256,128]{2,1,0:T(8,128)} copy(f32[2,256,128]{2,1,0:T(8,128)} %get-tuple-element.4) | data formatting | bytes 524288
  99.6 0.0 copy-done
  99.6 0.8 copy.10
Async XLA Ops:
  97.9 1.7 %copy-start = (f32[1024,128]{1,0:T(8,128)S(1)}, f32[1024,128]{1,0:T(8,128)}, u32[]{:S(2)}) copy-start(f32[1024,128]{1,0:T(8,128)} %get-tuple-element.5) | copy-start | bytes 1572868

commit v5 on v4

--- a/solution.py
+++ b/solution.py
@@ -239,60 +239,60 @@
     kept = lambda k: sh.at[k]
     spread = lambda k: Spread(k, xs.at[k], sb.at[k], sh.at[k])
 
+    spread_c = Spread(4, xc, cb, ch)
+    pair_a = ZPair(*views(2))
+    ring_0 = ZRing(*views(0))
+    ring_0.start()
     spread0 = spread(0)
-    ring_a = ZRing(*views(2))
-    ring_a.start()
-    pair0 = ZPair(*views(0))
-    spread_c = Spread(4, xc, cb, ch)
     spread2 = spread(2)
-    pair0.forward()
-    ring_a.advance()
+    pair_a.forward()
+    ring_0.advance()
     for copy in local[4:]:
         copy.wait()
     rings[0].start()
+    spread_c.arrived()
     spread0.arrived()
-    spread_c.arrived()
+    spread_c.finish()
+    ring_0.advance()
+    rings[1].start()
+    pair_a.finish()
+    wp[...] = partial(ch, factor(2))
+    sum_w = YSum(wp, wr)
     spread0.finish()
-    ring_a.advance()
-    rings[1].start()
-    pair0.finish()
+    spread2.arrived()
+    ring_0.advance()
+    spread2.finish()
+    rings[2].start()
+    ring_0.advance()
     part[4] = partial(kept(0), factor(0))
     sum_f = YSum(part.at[4], rs.at[4])
-    spread_c.finish()
-    spread2.arrived()
-    ring_a.advance()
-    spread2.finish()
-    ring_a.advance()
-    wp[...] = partial(ch, factor(2))
-    sum_w = YSum(wp, wr)
-    rings[0].advance()
+    az[1, z] = sum_w.total()
+    pair_w = ZPair(*views(1))
+    rings[3].start()
+    part[5] = partial(kept(2), factor(2))
     first = sum_f.total()
     xs[1] = first
     spread1 = spread(1)
     solved[0] = first.T
-    part[5] = partial(kept(2), factor(2))
-    az[1, z] = sum_w.total()
-    pair_w = ZPair(*views(1))
+    pair_w.forward()
+    rings[0].advance()
     rings[1].advance()
-    pair_w.forward()
-    rings[2].start()
-    rings[3].start()
-    rings[0].advance()
+    rings[2].advance()
     spread1.arrived()
+    pair_w.finish()
     spread1.finish()
-    rings[1].advance()
-    pair_w.finish()
     part[5] = part[5] - partial(kept(1), factor(1))
     sum_s = YSum(part.at[5], rs.at[5])
-    rings[2].advance()
+    rings[0].advance()
     rings[3].advance()
+    rings[1].advance()
     second = sum_s.total()
     xs[3] = second
     spread3 = spread(3)
     solved[1] = second.T
     rings[0].advance()
+    rings[2].advance()
     rings[1].advance()
-    rings[2].advance()
     rings[3].advance()
     rings[0].advance()
     part[0] = partial(kept(1), panel(0, 0))
@@ -301,15 +301,15 @@
     sums = []
     part[0] = part[0] + partial(kept(3), panel(0, 1))
     sums.append(YRelay(0))
+    rings[2].advance()
     rings[1].advance()
     part[1] = partial(kept(1), panel(1, 0)) + partial(kept(3), panel(1, 1))
     sums.append(YRelay(1))
-    rings[2].advance()
     rings[3].advance()
-    sums[0].forward()
     rings[2].advance()
     part[2] = partial(kept(1), panel(2, 0)) + partial(kept(3), panel(2, 1))
     sums.append(YRelay(2))
+    sums[0].forward()
     sums[1].forward()
     rings[3].advance()
     part[3] = partial(kept(1), panel(3, 0)) + partial(kept(3), panel(3, 1))
@@ -330,6 +330,7 @@
 def body(inv_diag, coupling, top_rhs, panel, rhs):
     hbm = pl.BlockSpec(memory_space=pltpu.HBM)
     vmem = pl.BlockSpec(memory_space=pltpu.VMEM)
+    operands = (jnp.swapaxes(inv_diag, 1, 2), coupling.T, top_rhs, jnp.swapaxes(panel, 1, 2), rhs)
     solved, trailing = pl.pallas_call(
         kernel,
         out_shape=(jax.ShapeDtypeStruct((2, MD, TD), F32), jax.ShapeDtypeStruct((CHUNKS * MD, TD), F32)),
@@ -356,8 +357,8 @@
             pltpu.SemaphoreType.DMA((N_LOCAL,)),
         ],
         compiler_params=pltpu.CompilerParams(
-            collective_id=0, has_side_effects=True, vmem_limit_bytes=62 * 1024 * 1024),
-    )(jnp.swapaxes(inv_diag, 1, 2), coupling.T, top_rhs, jnp.swapaxes(panel, 1, 2), rhs)
+            collective_id=0, has_side_effects=True, vmem_limit_bytes=32 * 1024 * 1024),
+    )(*(pltpu.with_memory_space_constraint(v, pltpu.HBM) for v in operands))
     return solved, trailing
 
 

time: 101 us -> 95.1 us (0.942)
  Pallas kernels: 97.2 us -> 92.8 us
  local copies, waits for them, and re-layouts: 2.52 us -> 1.5 us
    pallas_call x1, Pallas kernels: 97.2 us -> 92.8 us  [body(): pl.pallas_call(kernel, out_shape=(jax.ShapeDtypeStruct((2, MD, TD), F32),...]
    unnamed x4 -> x2, local copies, waits for them, and re-layouts: 2.52 us -> 1.5 us
where the time goes in v5:
time: 95.1 us; the launch traced here: 95 us
  Pallas kernels  92.8 us (98%)
  local copies, waits for them, and re-layouts  1.5 us (2%)
    pallas_call x1, Pallas kernels, body(): pl.pallas_call(kernel, out_shape=(jax.ShapeDtypeStruct((2, MD, TD), F32),...  92.8 us

profile of v5, /device:TPU:1, one launch (start us, length us, event | category | flops | bytes accessed | tf_op | source)
XLA Modules:
  0.0 95.0 jit_solution(1055119402876364016)
XLA Ops:
  0.6 92.8 %shard_map.68 = (f32[2,256,128]{2,1,0:T(8,128)S(1)}, f32[1024,128]{1,0:T(8,128)S(1)}) custom-call(f32[2,64,256]{2,1,0:T(8,128)} %bitcast.4, f32[64,256]{1,0:T(8,128)} %bitcast.5, f32[2,256,128]{2,1,0:T(8,128)} %top_h.1, f32[2,64,1024]{2,1,0:T(8,128)} %bitcast.3, f32[1024,128]{1,0:T(8,128)} %rhs_h.1), custom_call_target="tpu_custom_call" | custom-call | tf_op jit(solution)/shard_map/pallas_call | solution.py:334
  93.5 0.7 copy.9
  94.2 0.8 copy.10

commit v6 on v5

--- a/solution.py
+++ b/solution.py
@@ -12,7 +12,7 @@
 KD, MD, TD = 64, 256, 128
 KH = KD // 2
 CHUNKS = 4
-N_SEND, N_RECV, N_LOCAL = 29, 46, 9
+N_SEND, N_RECV, N_LOCAL = 37, 52, 9
 
 
 def split(v):
@@ -31,7 +31,7 @@
 
 
 def kernel(inv_h, cpl_h, top_h, pan_h, rhs_h, solved, trail,
-           az, pt, xs, sb, sh, cb, ch, xc, part, rs, wp, wr, top_v, rhs_v, send, recv, arrive, loc):
+           az, pt, xs, sb, sh, sbh, shh, cb, ch, xc, part, rs, wp, wr, top_v, rhs_v, send, recv, arrive, loc):
     row, col = lax.axis_index("row"), lax.axis_index("col")
     x, c = row // 2, row % 2
     y, z = col // NZ, col % NZ
@@ -169,40 +169,49 @@
         return lambda cc: pt[j, k, 4 * cc:4 * cc + 4]
 
     class YSum:
-        def __init__(self, mine, theirs):
-            self.mine, self.theirs, self.r = mine, theirs, fresh("recv")
-            s = group(theirs)
+        def __init__(self, mine, theirs, span=slice(None)):
+            self.mine, self.theirs, self.span, self.r = mine, theirs, span, fresh("recv")
+            s = group(theirs.at[:, span])
             for n, (yy, to) in enumerate(((y_op, to_y_op), (y_up, to_y_up), (y_dn, to_y_dn))):
-                push(mine.at[yy], theirs.at[n], to, s, self.r)
+                push(mine.at[yy, span], theirs.at[n, span], to, s, self.r)
 
         def total(self):
-            got(self.theirs, self.r)
-            return (self.mine[y] + self.theirs[0]) + (self.theirs[1] + self.theirs[2])
+            mine, theirs, span = self.mine, self.theirs, self.span
+            got(theirs.at[:, span], self.r)
+            return (mine[y, span] + theirs[0, span]) + (theirs[1, span] + theirs[2, span])
 
     class YRelay:
-        def __init__(self, j):
-            self.j, self.s = j, group(rs.at[j])
-            self.r = [fresh("recv") for _ in range(3)]
-            for h, to in enumerate((to_y_up, to_y_dn)):
-                push(part.at[j, y_op, halves[h]], rs.at[j, 2, halves[h]], to, self.s, self.r[h])
-            self.pass_on(0, y_up, 1, to_y_up)
-            self.pass_on(1, y_dn, 0, to_y_dn)
-
-        def pass_on(self, way, yy, h, to):
-            push(part.at[self.j, yy, halves[h]], rs.at[self.j, way, halves[h]], to, self.s, self.r[2])
+        def __init__(self, j, h):
+            self.j, self.h, self.s = j, h, group(rs.at[j, :, halves[h]])
+            self.r = [fresh("recv") for _ in range(2)]
+            self.via, self.to = ((y_up, to_y_up), (y_dn, to_y_dn))[h]
+            other, to_other = ((y_dn, to_y_dn), (y_up, to_y_up))[h]
+            push(part.at[j, y_op, halves[h]], rs.at[j, 2, halves[h]], self.to, self.s, self.r[0])
+            self.pass_on(1 - h, other, to_other)
+
+        def pass_on(self, way, yy, to):
+            half = halves[self.h]
+            push(part.at[self.j, yy, half], rs.at[self.j, way, half], to, self.s, self.r[1])
 
         def forward(self):
-            j = self.j
-            for h, yy, to in ((0, y_up, to_y_up), (1, y_dn, to_y_dn)):
-                got(rs.at[j, 2, halves[h]], self.r[h])
-                part[j, yy, halves[h]] = part[j, yy, halves[h]] + rs[j, 2, halves[h]]
-                self.pass_on(h, yy, h, to)
-
-        def store(self):
-            j = self.j
-            got(rs.at[j, pl.ds(0, 2)], self.r[2])
-            rows = pl.ds(j * MD, MD)
-            trail[rows] = rhs_v[rows] - (part[j, y] + (rs[j, 0] + rs[j, 1])).T
+            j, half = self.j, halves[self.h]
+            got(rs.at[j, 2, half], self.r[0])
+            part[j, self.via, half] = part[j, self.via, half] + rs[j, 2, half]
+            self.pass_on(self.h, self.via, self.to)
+
+        def finish(self):
+            got(rs.at[self.j, pl.ds(0, 2), halves[self.h]], self.r[1])
+
+    def store(j):
+        rows = pl.ds(j * MD, MD)
+        trail[rows] = rhs_v[rows] - (part[j, y] + (rs[j, 0] + rs[j, 1])).T
+
+    def first_part(j):
+        part[j] = partial(kept(1), panel(j, 0))
+
+    def second_part(j, h):
+        part[j, :, halves[h]] = part[j, :, halves[h]] + partial(shh.at[h], panel(j, 1))
+        return YRelay(j, h)
 
     local = []
 
@@ -262,13 +271,13 @@
     spread2.arrived()
     ring_0.advance()
     spread2.finish()
-    rings[2].start()
+    az[1, z] = sum_w.total()
+    pair_w = ZPair(*views(1))
     ring_0.advance()
     part[4] = partial(kept(0), factor(0))
     sum_f = YSum(part.at[4], rs.at[4])
-    az[1, z] = sum_w.total()
-    pair_w = ZPair(*views(1))
-    rings[3].start()
+    rings[0].advance()
+    rings[2].start()
     part[5] = partial(kept(2), factor(2))
     first = sum_f.total()
     xs[1] = first
@@ -277,47 +286,62 @@
     pair_w.forward()
     rings[0].advance()
     rings[1].advance()
-    rings[2].advance()
+    rings[3].start()
     spread1.arrived()
     pair_w.finish()
     spread1.finish()
     part[5] = part[5] - partial(kept(1), factor(1))
-    sum_s = YSum(part.at[5], rs.at[5])
+    sums_s = [YSum(part.at[5], rs.at[5], half) for half in halves]
     rings[0].advance()
-    rings[3].advance()
     rings[1].advance()
-    second = sum_s.total()
-    xs[3] = second
-    spread3 = spread(3)
-    solved[1] = second.T
+    rings[2].advance()
+    spreads3 = []
+    for h in range(2):
+        xs[3, halves[h]] = sums_s[h].total()
+        spreads3.append(Spread((3, 5)[h], xs.at[3, halves[h]], sbh.at[h], shh.at[h]))
+    solved[1] = xs[3].T
     rings[0].advance()
-    rings[2].advance()
     rings[1].advance()
     rings[3].advance()
-    rings[0].advance()
-    part[0] = partial(kept(1), panel(0, 0))
-    spread3.arrived()
-    spread3.finish()
-    sums = []
-    part[0] = part[0] + partial(kept(3), panel(0, 1))
-    sums.append(YRelay(0))
+    first_part(0)
     rings[2].advance()
+    spreads3[0].arrived()
+    spreads3[1].arrived()
+    spreads3[0].finish()
+    relays = [second_part(0, 0)]
     rings[1].advance()
-    part[1] = partial(kept(1), panel(1, 0)) + partial(kept(3), panel(1, 1))
-    sums.append(YRelay(1))
     rings[3].advance()
+    spreads3[1].finish()
+    relays.append(second_part(0, 1))
     rings[2].advance()
-    part[2] = partial(kept(1), panel(2, 0)) + partial(kept(3), panel(2, 1))
-    sums.append(YRelay(2))
-    sums[0].forward()
-    sums[1].forward()
+    first_part(1)
+    relays.append(second_part(1, 0))
+    relays.append(second_part(1, 1))
+    relays[0].forward()
     rings[3].advance()
-    part[3] = partial(kept(1), panel(3, 0)) + partial(kept(3), panel(3, 1))
-    sums.append(YRelay(3))
-    sums[2].forward()
-    sums[3].forward()
-    for s in sums:
-        s.store()
+    relays[1].forward()
+    rings[2].advance()
+    first_part(2)
+    relays[2].forward()
+    relays.append(second_part(2, 0))
+    relays.append(second_part(2, 1))
+    relays[3].forward()
+    rings[3].advance()
+    first_part(3)
+    relays.append(second_part(3, 0))
+    relays.append(second_part(3, 1))
+    for relay in relays[4:]:
+        relay.forward()
+    for relay in relays[:4]:
+        relay.finish()
+    store(0)
+    store(1)
+    for relay in relays[4:6]:
+        relay.finish()
+    store(2)
+    for relay in relays[6:]:
+        relay.finish()
+    store(3)
     for ref, i, when in drains:
         wait = remote(ref, ref, to_core, i, recv.at[0]).wait_send
         if when is None:
@@ -340,8 +364,10 @@
             pltpu.VMEM((3, NZ, KD, MD), F32),
             pltpu.VMEM((CHUNKS, 2, NZ, KD, MD), F32),
             pltpu.VMEM((4, TD, MD), F32),
-            pltpu.VMEM((4, 2, NY, TD, MD), F32),
-            pltpu.VMEM((4, 2, 2, NY, TD, MD), BF16),
+            pltpu.VMEM((3, 2, NY, TD, MD), F32),
+            pltpu.VMEM((3, 2, 2, NY, TD, MD), BF16),
+            pltpu.VMEM((2, 2, NY, TD // 2, MD), F32),
+            pltpu.VMEM((2, 2, 2, NY, TD // 2, MD), BF16),
             pltpu.VMEM((2, NY, KD, MD), F32),
             pltpu.VMEM((2, 2, NY, KD, MD), BF16),
             pltpu.VMEM((KD, MD), F32),
@@ -353,7 +379,7 @@
             pltpu.VMEM((CHUNKS * MD, TD), F32),
             pltpu.SemaphoreType.DMA((N_SEND,)),
             pltpu.SemaphoreType.DMA((N_RECV,)),
-            pltpu.SemaphoreType.DMA((5, NY)),
+            pltpu.SemaphoreType.DMA((6, NY)),
             pltpu.SemaphoreType.DMA((N_LOCAL,)),
         ],
         compiler_params=pltpu.CompilerParams(

time: 95.1 us -> 92.5 us (0.973)
  Pallas kernels: 92.8 us -> 90.3 us
    pallas_call x1, Pallas kernels: 92.8 us -> 90.3 us  [body(): pl.pallas_call(kernel, out_shape=(jax.ShapeDtypeStruct((2, MD, TD), F32),...]
where the time goes in v6:
time: 92.5 us; the launch traced here: 92.4 us
  Pallas kernels  90.3 us (98%)
  local copies, waits for them, and re-layouts  1.5 us (2%)
    pallas_call x1, Pallas kernels, body(): pl.pallas_call(kernel, out_shape=(jax.ShapeDtypeStruct((2, MD, TD), F32),...  90.3 us

profile of v6, /device:TPU:1, one launch (start us, length us, event | category | flops | bytes accessed | tf_op | source)
XLA Modules:
  0.0 92.4 jit_solution(1113444473254475475)
XLA Ops:
  0.6 90.3 %shard_map.68 = (f32[2,256,128]{2,1,0:T(8,128)S(1)}, f32[1024,128]{1,0:T(8,128)S(1)}) custom-call(f32[2,64,256]{2,1,0:T(8,128)} %bitcast.4, f32[64,256]{1,0:T(8,128)} %bitcast.5, f32[2,256,128]{2,1,0:T(8,128)} %top_h.1, f32[2,64,1024]{2,1,0:T(8,128)} %bitcast.3, f32[1024,128]{1,0:T(8,128)} %rhs_h.1), custom_call_target="tpu_custom_call" | custom-call | tf_op jit(solution)/shard_map/pallas_call | solution.py:358
  90.9 0.7 copy.9
  91.6 0.8 copy.10

commit v7 on v6

--- a/solution.py
+++ b/solution.py
@@ -279,11 +279,11 @@
     rings[0].advance()
     rings[2].start()
     part[5] = partial(kept(2), factor(2))
+    pair_w.forward()
     first = sum_f.total()
     xs[1] = first
     spread1 = spread(1)
     solved[0] = first.T
-    pair_w.forward()
     rings[0].advance()
     rings[1].advance()
     rings[3].start()
@@ -295,6 +295,7 @@
     rings[0].advance()
     rings[1].advance()
     rings[2].advance()
+    rings[3].advance()
     spreads3 = []
     for h in range(2):
         xs[3, halves[h]] = sums_s[h].total()
@@ -302,20 +303,19 @@
     solved[1] = xs[3].T
     rings[0].advance()
     rings[1].advance()
-    rings[3].advance()
     first_part(0)
     rings[2].advance()
     spreads3[0].arrived()
-    spreads3[1].arrived()
     spreads3[0].finish()
     relays = [second_part(0, 0)]
+    spreads3[1].arrived()
+    rings[3].advance()
     rings[1].advance()
-    rings[3].advance()
     spreads3[1].finish()
     relays.append(second_part(0, 1))
-    rings[2].advance()
     first_part(1)
     relays.append(second_part(1, 0))
+    rings[2].advance()
     relays.append(second_part(1, 1))
     relays[0].forward()
     rings[3].advance()

time: 92.5 us -> 91.4 us (0.988)
  Pallas kernels: 90.3 us -> 88.6 us
    pallas_call x1, Pallas kernels: 90.3 us -> 88.6 us  [body(): pl.pallas_call(kernel, out_shape=(jax.ShapeDtypeStruct((2, MD, TD), F32),...]
where the time goes in v7:
time: 91.4 us; the launch traced here: 90.7 us
  Pallas kernels  88.6 us (97%)
  local copies, waits for them, and re-layouts  1.5 us (2%)
    pallas_call x1, Pallas kernels, body(): pl.pallas_call(kernel, out_shape=(jax.ShapeDtypeStruct((2, MD, TD), F32),...  88.6 us

profile of v7, /device:TPU:1, one launch (start us, length us, event | category | flops | bytes accessed | tf_op | source)
XLA Modules:
  0.0 90.7 jit_solution(4589335293383565562)
XLA Ops:
  0.6 88.6 %shard_map.68 = (f32[2,256,128]{2,1,0:T(8,128)S(1)}, f32[1024,128]{1,0:T(8,128)S(1)}) custom-call(f32[2,64,256]{2,1,0:T(8,128)} %bitcast.4, f32[64,256]{1,0:T(8,128)} %bitcast.5, f32[2,256,128]{2,1,0:T(8,128)} %top_h.1, f32[2,64,1024]{2,1,0:T(8,128)} %bitcast.3, f32[1024,128]{1,0:T(8,128)} %rhs_h.1), custom_call_target="tpu_custom_call" | custom-call | tf_op jit(solution)/shard_map/pallas_call | solution.py:358
  89.2 0.7 copy.9
  89.9 0.8 copy.10

commit v8 on v7

--- a/solution.py
+++ b/solution.py
@@ -316,8 +316,8 @@
     first_part(1)
     relays.append(second_part(1, 0))
     rings[2].advance()
+    relays[0].forward()
     relays.append(second_part(1, 1))
-    relays[0].forward()
     rings[3].advance()
     relays[1].forward()
     rings[2].advance()

time: 91.4 us -> 91.4 us (level)
  no operation moved by 1% of the time
where the time goes in v8:
time: 91.4 us; the launch traced here: 90.7 us
  Pallas kernels  88.6 us (97%)
  local copies, waits for them, and re-layouts  1.5 us (2%)
    pallas_call x1, Pallas kernels, body(): pl.pallas_call(kernel, out_shape=(jax.ShapeDtypeStruct((2, MD, TD), F32),...  88.6 us

profile of v8, /device:TPU:1, one launch (start us, length us, event | category | flops | bytes accessed | tf_op | source)
XLA Modules:
  0.0 90.7 jit_solution(12536751179594057501)
XLA Ops:
  0.6 88.6 %shard_map.68 = (f32[2,256,128]{2,1,0:T(8,128)S(1)}, f32[1024,128]{1,0:T(8,128)S(1)}) custom-call(f32[2,64,256]{2,1,0:T(8,128)} %bitcast.4, f32[64,256]{1,0:T(8,128)} %bitcast.5, f32[2,256,128]{2,1,0:T(8,128)} %top_h.1, f32[2,64,1024]{2,1,0:T(8,128)} %bitcast.3, f32[1024,128]{1,0:T(8,128)} %rhs_h.1), custom_call_target="tpu_custom_call" | custom-call | tf_op jit(solution)/shard_map/pallas_call | solution.py:358
  89.2 0.7 copy.9
  89.9 0.8 copy.10
